TPU v7x, 256 devices: a whole 4x4x8 slice. The times are simulated.
256 devices in a mesh: seq: 16 (over x, y_hi, core), tensor: 16 (over y_lo, z).
Axes of the slice: x: 4, y: 4 (y_hi: 2, y_lo: 2; y = y_hi * 2 + y_lo), z: 8, core: 2. Of those that a mesh axis runs over, the one named last changes fastest.
Arguments:
- ssd_input: bfloat16 [6144, 8192], P('seq', 'tensor'), may hold values from -6 to 6
- gate_input: bfloat16 [6144, 8192], P('seq', 'tensor'), may hold values from -6 to 6
- state_maps: bfloat16 [6144, 2, 2048], P('seq', None, 'tensor'), may hold values from -2 to 2
- step_raw: float32 [6144, 64], P('seq', 'tensor'), may hold values from -3 to 3
- step_bias: float32 [64], P('tensor'), may hold values from -1 to 0
- decay_rate: float32 [64], P('tensor'), may hold values from 0.00043402778 to 0.1, as said below
- skip_gain: float32 [64], P('tensor'), may hold values from 0.5 to 1.5
- norm_gain: float32 [8192], P('tensor'), may hold values from 0.1 to 1.9
- out_weight: bfloat16 [4096, 8192], P(None, 'tensor'), may hold values from -0.176776695 to 0.176776695
- reward_head: float32 [4096], replicated, may hold values from -0.25 to 0.25
- traj_lengths: int32 [32], replicated, may hold values from 1 to 1152, 6144 in all
- step_pairs: int32 [6144], replicated, may hold values from 0 to 6143, each once
Outputs:
- rewards: float32 [6144], P('seq')
- grad_input: bfloat16 [6144, 8192], P('seq', 'tensor')
- grad_gate: bfloat16 [6144, 8192], P('seq', 'tensor')
- grad_maps: bfloat16 [6144, 2, 2048], P('seq', None, 'tensor')
- grad_step: float32 [6144, 64], P('seq', 'tensor')
Inputs may be any that keep to these rules, and one draw needn't show every extreme that they name: `traj_lengths`: trajectory lengths sum to 6144; the longest is exactly 1152. A permutation of the token positions; step_pairs[2k] is the chosen and step_pairs[2k+1] the rejected step of pair k. `decay_rate`: positive decay rates.
All inputs are finite; a program needn't handle non-finite values.
Results may differ from a plain program's by a relative error of at most 0.006.
Values may be sent and summed in bfloat16 or wider, within the bound.
A program may use at most 64 MiB of HBM per device.

v0:
```python
import jax
import jax.numpy as jnp
from jax import lax
from jax.experimental import pallas as pl
from jax.experimental.pallas import tpu as pltpu
from jax.sharding import PartitionSpec as P

STATE = 128
BLOCK = 128

norm_eps = 1e-05
loss_scale = 64.0
longest = 1152
MESH = pl.DeviceIdType.MESH
HIGH = lax.Precision.HIGHEST
NT = ((1,), (1,))
NN = ((1,), (0,))
TN = ((0,), (0,))


def dot(left, right, dims, precision=None):
    return lax.dot_general(
        left, right, (dims, ((), ())), preferred_element_type=jnp.float32, precision=precision
    )


def iota(shape, axis):
    return lax.broadcasted_iota(jnp.int32, shape, axis)


def layer_kernel(
    x_ref,
    z_ref,
    b_ref,
    c_ref,
    raw_ref,
    bias_ref,
    rate_ref,
    wide_ref,
    weight_ref,
    head_ref,
    length_row_ref,
    length_col_ref,
    pairs_ref,
    reward_out,
    dx_ref,
    dz_ref,
    db_ref,
    dc_ref,
    dstep_ref,
    weight,
    columns,
    decays,
    scores,
    y_all,
    carried_all,
    state_in,
    mixed,
    weighted_x,
    mate_all,
    sign_all,
    state_out,
    state_far,
    grad_out,
    grad_far,
    dy_all,
    faded_dy,
    dx_all,
    db_all,
    sums,
    column_sums,
    back,
    rewards,
    first,
    moving,
    swap_out,
    swap_in,
    hidden,
    own_stats,
    far_stats,
    own_reward,
    weight_sem,
    state_send,
    state_recv,
    grad_send,
    grad_recv,
    reduce_send,
    reduce_recv,
    swap_send,
    swap_recv,
    gather_send,
    gather_recv,
    stats_send,
    stats_recv,
    reward_send,
    reward_recv,
):
    seq, tensor = lax.axis_index("seq"), lax.axis_index("tensor")
    seq_count, tensor_count = lax.axis_size("seq"), lax.axis_size("tensor")
    chips = tensor_count // 2
    place, side = lax.rem(tensor, chips), tensor // chips
    base = side * chips
    up = (seq, base + lax.rem(place + 1, chips))
    down = (seq, base + lax.rem(place + chips - 1, chips))
    across = (seq, (1 - side) * chips + place)
    ways = (up, down)
    tokens, channels = x_ref.shape
    model_width = weight.shape[0]
    half = hidden.shape[-1]
    pieces = hidden.shape[2]
    piece = tokens // pieces
    width = channels // (raw_ref.shape[0] // 2)
    heads = channels // width
    blocks = tokens // BLOCK
    reach = state_far.shape[0]
    pair_tiles = pairs_ref.shape[1] // BLOCK

    weight_copy = pltpu.make_async_copy(weight_ref, weight, weight_sem)
    weight_copy.start()
    barrier = pltpu.get_barrier_semaphore()

    def greet_tensor(k, _):
        other = lax.rem(tensor + k, tensor_count)
        pl.semaphore_signal(barrier, inc=1, device_id=(seq, other), device_id_type=MESH)
        return 0

    def greet_seq(k, _):
        other = lax.rem(seq + k, seq_count)
        pl.semaphore_signal(barrier, inc=1, device_id=(other, tensor), device_id_type=MESH)
        return 0

    lax.fori_loop(1, tensor_count, greet_tensor, 0)
    lax.fori_loop(1, seq_count, greet_seq, 0)

    def span(tb):
        return slice(tb * BLOCK, (tb + 1) * BLOCK)

    def lanes(h):
        return slice(h * width, (h + 1) * width)

    pre = raw_ref[...] + bias_ref[...]
    step = jnp.maximum(pre, 0.0) + jnp.log1p(jnp.exp(-jnp.abs(pre)))
    exponent = -step * rate_ref[...]
    square = (tokens, tokens)
    upto = (iota(square, 0) <= iota(square, 1)).astype(jnp.float32)
    cumulative = dot(exponent, upto, NN, HIGH)
    count = length_row_ref.shape[1]
    openings = jnp.sum(
        jnp.where(
            iota((count, count), 1) < iota((count, count), 0),
            length_row_ref[...].astype(jnp.float32),
            0.0,
        ),
        axis=1,
        keepdims=True,
    )
    position = (iota((count, tokens), 1) + seq * tokens).astype(jnp.float32)
    block_start = (iota((count, tokens), 0) * 0 + seq * tokens).astype(jnp.float32)
    segment = jnp.sum(
        jnp.where((openings <= position) & (openings >= block_start), 1.0, 0.0),
        axis=0,
        keepdims=True,
    )
    last_segment = segment[:, tokens - 1 :]
    last_cumulative = cumulative[:, tokens - 1 :]
    end_weight = jnp.where(
        jnp.broadcast_to(segment == last_segment, step.shape),
        jnp.exp(last_cumulative - cumulative),
        0.0,
    )
    end_weight = end_weight * step
    first_weight = jnp.where(
        jnp.broadcast_to(segment == 0.0, step.shape), jnp.exp(cumulative), 0.0
    )
    through = jnp.where(last_segment == 0.0, jnp.exp(last_cumulative), 0.0)
    segment_rows = jnp.broadcast_to(segment, step.shape)
    columns[...] = jnp.concatenate(
        [
            end_weight,
            first_weight,
            cumulative,
            segment_rows,
            jnp.zeros((BLOCK - 32, tokens), jnp.float32),
        ],
        axis=0,
    ).T

    def column(kind, h, tb):
        return columns[span(tb), kind * 8 + h : kind * 8 + h + 1]

    def expanded(kind, tb):
        return jnp.concatenate(
            [jnp.broadcast_to(column(kind, h, tb), (BLOCK, width)) for h in range(heads)], axis=1
        )

    through_wide = jnp.concatenate(
        [jnp.broadcast_to(through[h : h + 1], (1, width)) for h in range(heads)], axis=1
    )
    through_high = through_wide.astype(jnp.bfloat16).astype(jnp.float32)
    tail_shape = (16, channels)
    through_rows = jnp.where(
        iota(tail_shape, 0) == 0,
        through_high,
        jnp.where(iota(tail_shape, 0) == 1, through_wide - through_high, 0.0),
    ).astype(jnp.bfloat16)

    def far_copy(source, target, send, recv, distance, direction):
        return pltpu.make_async_remote_copy(
            src_ref=source,
            dst_ref=target.at[distance - 1],
            send_sem=send.at[distance - 1],
            recv_sem=recv.at[distance - 1],
            device_id=(lax.rem(seq + seq_count + direction * distance, seq_count), tensor),
            device_id_type=MESH,
        )

    def state_copy(distance):
        return far_copy(state_out, state_far, state_send, state_recv, distance, 1)

    def grad_copy(distance):
        return far_copy(grad_out, grad_far, grad_send, grad_recv, distance, -1)

    def gathered(far):
        total, carry = None, None
        for k in range(reach):
            value = far[k, 0:STATE].astype(jnp.float32)
            passed = far[k, STATE : STATE + 1].astype(jnp.float32) + far[
                k, STATE + 1 : STATE + 2
            ].astype(jnp.float32)
            if total is None:
                total, carry = value, passed
            else:
                total = total + carry * value
                carry = carry * passed
        return total

    for tb in range(blocks):
        weighted_x[span(tb)] = (
            x_ref[span(tb)].astype(jnp.float32) * expanded(0, tb)
        ).astype(jnp.bfloat16)
    state_out[0:STATE] = dot(b_ref[...], weighted_x[...], TN).astype(jnp.bfloat16)
    state_out[STATE:] = through_rows
    pl.semaphore_wait(barrier, tensor_count + seq_count - 2)
    for distance in range(1, reach + 1):
        state_copy(distance).start()

    for tb in range(blocks):
        reached = (tb + 1) * BLOCK
        score = dot(c_ref[span(tb)], b_ref[0:reached], NT)
        scores[span(tb), 0:reached] = score
        shape = (BLOCK, reached)
        allowed = (column(3, 0, tb) == segment[:, 0:reached]) & (
            iota(shape, 1) <= iota(shape, 0) + tb * BLOCK
        )
        for h in range(heads):
            spread = column(2, h, tb) - cumulative[h : h + 1, 0:reached]
            decay = jnp.exp(jnp.where(allowed, spread, -1e30)) * step[h : h + 1, 0:reached]
            decays[h, span(tb), 0:reached] = decay
            y_all[span(tb), lanes(h)] = dot(
                (decay * score).astype(jnp.bfloat16), x_ref[0:reached, lanes(h)], NN
            )

    reward_row = head_ref[...]
    high = reward_row.astype(jnp.bfloat16).astype(jnp.float32)
    rest = reward_row - high
    middle = rest.astype(jnp.bfloat16).astype(jnp.float32)
    term = iota((8, model_width), 0)
    terms = jnp.where(
        term == 0,
        high,
        jnp.where(term == 1, middle, jnp.where(term == 2, rest - middle, 0.0)),
    ).astype(jnp.bfloat16)
    weight_copy.wait()
    reward_channels = jnp.sum(dot(terms, weight[...], NN), axis=0, keepdims=True)

    tile = (BLOCK, BLOCK)
    unroll = 4
    for tb in range(blocks):
        token = iota(tile, 0) + (seq * tokens + tb * BLOCK)

        def find(i, total):
            for k in range(unroll):
                start = pl.multiple_of((i * unroll + k) * BLOCK, BLOCK)
                row = pairs_ref[0:1, pl.ds(start, BLOCK)]
                order = (iota(tile, 1) + start).astype(jnp.float32)
                total = total + jnp.where(row == token, order, 0.0)
            return total

        zero = jnp.zeros(tile, jnp.float32)
        order = jnp.sum(
            lax.fori_loop(0, pair_tiles // unroll, find, zero), axis=1, keepdims=True
        )
        odd = order - 2.0 * jnp.floor(order * 0.5)
        other = jnp.broadcast_to(order + 1.0 - 2.0 * odd, tile)

        def fetch(i, total):
            for k in range(unroll):
                start = pl.multiple_of((i * unroll + k) * BLOCK, BLOCK)
                row = pairs_ref[0:1, pl.ds(start, BLOCK)].astype(jnp.float32)
                order = (iota(tile, 1) + start).astype(jnp.float32)
                total = total + jnp.where(other == order, row, 0.0)
            return total

        mate = jnp.sum(
            lax.fori_loop(0, pair_tiles // unroll, fetch, zero), axis=1, keepdims=True
        )
        mate_all[span(tb)] = jnp.broadcast_to(mate, tile)
        sign_all[span(tb)] = jnp.broadcast_to(2.0 * odd - 1.0, tile)

    for distance in range(1, reach + 1):
        state_copy(distance).wait_recv()
    state_in[...] = gathered(state_far)
    incoming = state_in[...].astype(jnp.bfloat16)
    gain, skip = wide_ref[0:1], wide_ref[1:2]

    def gating(tb):
        y = y_all[span(tb)]
        z = z_ref[span(tb)].astype(jnp.float32)
        sig = 1.0 / (1.0 + jnp.exp(-z))
        silu = z * sig
        gated = y * silu
        mean_square = jnp.sum(gated * gated, axis=1, keepdims=True) / channels
        return y, z, sig, silu, gated, lax.rsqrt(mean_square + norm_eps)

    for tb in range(blocks):
        carried = expanded(1, tb) * dot(c_ref[span(tb)], incoming, NN)
        carried_all[span(tb)] = carried
        y_all[span(tb)] = (
            y_all[span(tb)] + carried + skip * x_ref[span(tb)].astype(jnp.float32)
        )
        _, _, _, _, gated, inverse = gating(tb)
        mixed[span(tb)] = (gated * inverse * gain).astype(jnp.bfloat16)

    def chunk(way, distance):
        move = distance if way == 1 else chips - distance
        return lax.rem(place + move, chips)

    def rows(index, way):
        return pl.ds(pl.multiple_of((index * 2 + way) * half, half), half)

    def own_part(way, distance):
        return lax.dot_general(
            mixed[...],
            weight[rows(chunk(way, distance), way), :],
            (((1,), (1,)), ((), ())),
            preferred_element_type=jnp.float32,
        )

    def reduce_copy(way, step, j, source):
        return pltpu.make_async_remote_copy(
            src_ref=source,
            dst_ref=moving.at[way, step, j],
            send_sem=reduce_send.at[way, step, j],
            recv_sem=reduce_recv.at[way, step, j],
            device_id=ways[way],
            device_id_type=MESH,
        )

    def reduce_source(way, step, j):
        return first.at[way, j] if step is None else moving.at[way, step, j]

    for way in range(2):
        part = own_part(way, 1)
        for j in range(pieces):
            first[way, j] = part[j * piece : (j + 1) * piece].astype(jnp.bfloat16)
    for j in range(pieces):
        for way in range(2):
            reduce_copy(way, 0, j, first.at[way, j]).start()

    along = lax.dot_general(
        jnp.broadcast_to(reward_channels, (8, channels)),
        mixed[...].astype(jnp.float32),
        (((1,), (1,)), ((), ())),
        preferred_element_type=jnp.float32,
        precision=lax.Precision.HIGHEST,
    )

    def reduce_step(step, _):
        parts = [own_part(way, step + 2) for way in range(2)]
        for j in range(pieces):
            for way in range(2):
                reduce_copy(way, step, j, moving.at[way, step, j]).wait_recv()
                moving[way, step, j] = (
                    moving[way, step, j].astype(jnp.float32)
                    + parts[way][j * piece : (j + 1) * piece]
                ).astype(jnp.bfloat16)
                reduce_copy(way, step + 1, j, moving.at[way, step, j]).start()
        return 0

    lax.fori_loop(0, chips - 2, reduce_step, 0)

    def swap_copy(way, j):
        return pltpu.make_async_remote_copy(
            src_ref=swap_out.at[way, j],
            dst_ref=swap_in.at[way, j],
            send_sem=swap_send.at[way, j],
            recv_sem=swap_recv.at[way, j],
            device_id=across,
            device_id_type=MESH,
        )

    last = chips - 2
    parts = [own_part(way, chips) for way in range(2)]
    for j in range(pieces):
        for way in range(2):
            reduce_copy(way, last, j, moving.at[way, last, j]).wait_recv()
            swap_out[way, j] = (
                moving[way, last, j].astype(jnp.float32) + parts[way][j * piece : (j + 1) * piece]
            ).astype(jnp.bfloat16)
            swap_copy(way, j).start()

    def gather_copy(way, step, j):
        index = chunk(way, chips + step if way == 1 else step)
        return pltpu.make_async_remote_copy(
            src_ref=hidden.at[index, way, j],
            dst_ref=hidden.at[index, way, j],
            send_sem=gather_send.at[way, step, j],
            recv_sem=gather_recv.at[way, step, j],
            device_id=ways[way],
            device_id_type=MESH,
        )

    for j in range(pieces):
        for way in range(2):
            swap_copy(way, j).wait_recv()
            hidden[place, way, j] = (
                swap_out[way, j].astype(jnp.float32) + swap_in[way, j].astype(jnp.float32)
            ).astype(jnp.bfloat16)
            gather_copy(way, 0, j).start()

    ones = jnp.ones((8, half), jnp.float32)
    squares = []
    for j in range(pieces):
        total = None
        for way in range(2):
            value = hidden[place, way, j].astype(jnp.float32)
            total = value * value if total is None else total + value * value
        squares.append(
            lax.dot_general(
                ones,
                total,
                (((1,), (1,)), ((), ())),
                preferred_element_type=jnp.float32,
                precision=lax.Precision.HIGHEST,
            )
        )
    is_along = lax.broadcasted_iota(jnp.int32, (8, tokens), 0) == 0
    own_stats[...] = jnp.where(is_along, along, 0.5 * jnp.concatenate(squares, axis=1))

    def stats_copy(k):
        return pltpu.make_async_remote_copy(
            src_ref=own_stats,
            dst_ref=far_stats.at[k],
            send_sem=stats_send.at[k],
            recv_sem=stats_recv.at[k],
            device_id=(seq, lax.rem(tensor + k, tensor_count)),
            device_id_type=MESH,
        )

    def reward_copy(k):
        return pltpu.make_async_remote_copy(
            src_ref=own_reward,
            dst_ref=rewards.at[seq],
            send_sem=reward_send.at[k],
            recv_sem=reward_recv.at[k],
            device_id=(lax.rem(seq + k, seq_count), tensor),
            device_id_type=MESH,
        )

    def start_stats(k, _):
        stats_copy(k).start()
        return 0

    lax.fori_loop(1, tensor_count, start_stats, 0)

    def back_part(index, way):
        return lax.dot_general(
            hidden[index, way].reshape(tokens, half),
            weight[rows(index, way), :],
            (((1,), (0,)), ((), ())),
            preferred_element_type=jnp.float32,
        )

    back[...] = back_part(place, 0) + back_part(place, 1)

    def gather_step(step, _):
        for j in range(pieces):
            for way in range(2):
                gather_copy(way, step, j).wait_recv()
                gather_copy(way, step + 1, j).start()
        back[...] += back_part(chunk(0, step + 1), 0) + back_part(chunk(1, step + 1), 1)
        return 0

    lax.fori_loop(0, 2, gather_step, 0)

    def add_stats(k, total):
        stats_copy(k).wait_recv()
        return total + far_stats[k]

    stats = lax.fori_loop(1, tensor_count, add_stats, own_stats[...])
    scale = jnp.sqrt(stats[1:2] / model_width + norm_eps)
    own_reward[...] = jnp.broadcast_to(stats[0:1] / scale, own_reward.shape)
    rewards[seq] = own_reward[...]

    def start_reward(k, _):
        reward_copy(k).start()
        return 0

    lax.fori_loop(1, seq_count, start_reward, 0)
    lax.fori_loop(2, chips - 2, gather_step, 0)
    for j in range(pieces):
        for way in range(2):
            gather_copy(way, last, j).wait_recv()
    back[...] += back_part(chunk(0, chips - 1), 0) + back_part(chunk(1, chips - 1), 1)

    def end_reward(k, _):
        reward_copy(k).wait()
        return 0

    lax.fori_loop(1, seq_count, end_reward, 0)

    def end_stats(k, _):
        stats_copy(k).wait_send()
        return 0

    lax.fori_loop(1, tensor_count, end_stats, 0)

    def end_ring(step, _):
        for j in range(pieces):
            for way in range(2):
                reduce_copy(way, step, j, first.at[way, j]).wait_send()
                gather_copy(way, step, j).wait_send()
        return 0

    lax.fori_loop(0, chips - 1, end_ring, 0)
    for j in range(pieces):
        for way in range(2):
            swap_copy(way, j).wait_send()

    reward_out[...] = own_reward[...]

    facts = jnp.concatenate(
        [stats, jnp.broadcast_to(scale, stats.shape), own_reward[...]]
        + [jnp.zeros((BLOCK - 24, tokens), jnp.float32)],
        axis=0,
    ).T
    lane = iota(tile, 1)
    for tb in range(blocks):
        mate = mate_all[span(tb)].astype(jnp.int32)
        sign = sign_all[span(tb), 0:1]

        def look(i, total):
            for k in range(blocks):
                row = rewards[i, 0:1, k * BLOCK : (k + 1) * BLOCK]
                total = total + jnp.where(mate == lane + (i * tokens + k * BLOCK), row, 0.0)
            return total

        mate_reward = jnp.sum(
            lax.fori_loop(0, seq_count, look, jnp.zeros(tile, jnp.float32)), axis=1, keepdims=True
        )
        own_along = facts[span(tb), 0:1]
        own_scale = facts[span(tb), 8:9]
        push = sign * (facts[span(tb), 16:17] - mate_reward)
        pair_grad = sign * (loss_scale / (1.0 + jnp.exp(-push)))
        y, z, sig, silu, gated, inverse = gating(tb)
        d_gained = gain * (
            (pair_grad / own_scale)
            * (reward_channels - (own_along / (model_width * own_scale * own_scale)) * back[span(tb)])
        )
        shared = jnp.sum(gated * d_gained, axis=1, keepdims=True) / channels
        d_gated = inverse * d_gained - gated * (inverse * inverse * inverse * shared)
        dz_ref[span(tb)] = (d_gated * y * (sig * (1.0 + z * (1.0 - sig)))).astype(jnp.bfloat16)
        dy = d_gated * silu
        dy_all[span(tb)] = dy.astype(jnp.bfloat16)
        faded_dy[span(tb)] = (dy * expanded(1, tb)).astype(jnp.bfloat16)
        dx_all[span(tb)] = skip * dy
        product = dy * carried_all[span(tb)]
        total = jnp.zeros(tile, jnp.float32)
        for h in range(heads):
            total = total + jnp.where(
                lane == h, jnp.sum(product[:, lanes(h)], axis=1, keepdims=True), 0.0
            )
        sums[span(tb)] = total
    grad_out[0:STATE] = dot(c_ref[...], faded_dy[...], TN).astype(jnp.bfloat16)
    grad_out[STATE:] = through_rows
    for distance in range(1, reach + 1):
        grad_copy(distance).start()

    column_sums[...] = jnp.zeros_like(column_sums)
    db_all[...] = jnp.zeros_like(db_all)
    for tb in range(blocks):
        reached = (tb + 1) * BLOCK
        score = scores[span(tb), 0:reached]
        d_score = None
        row_sums = sums[span(tb)]
        for h in range(heads):
            dy = dy_all[span(tb), lanes(h)]
            decay = decays[h, span(tb), 0:reached]
            d_decayed = decay * dot(dy, x_ref[0:reached, lanes(h)], NT)
            d_score = d_decayed if d_score is None else d_score + d_decayed
            weighed = d_decayed * score
            row_sums = row_sums + jnp.where(
                lane == h, jnp.sum(weighed, axis=1, keepdims=True), 0.0
            )
            column_sums[h : h + 1, 0:reached] += jnp.sum(weighed, axis=0, keepdims=True)
            dx_all[0:reached, lanes(h)] += dot((decay * score).astype(jnp.bfloat16), dy, TN)
        sums[span(tb)] = row_sums
        d_score = d_score.astype(jnp.bfloat16)
        dc_ref[span(tb)] = (
            dot(d_score, b_ref[0:reached], NN) + dot(faded_dy[span(tb)], incoming, NT)
        ).astype(jnp.bfloat16)
        db_all[0:reached] += dot(d_score, c_ref[span(tb)], TN)

    for distance in range(1, reach + 1):
        grad_copy(distance).wait_recv()
    grad_end = gathered(grad_far)
    crossing = jnp.sum(grad_end * state_in[...], axis=0, keepdims=True)
    grad_end = grad_end.astype(jnp.bfloat16)
    for tb in range(blocks):
        d_weighted = expanded(0, tb) * dot(b_ref[span(tb)], grad_end, NN)
        dx_ref[span(tb)] = (dx_all[span(tb)] + d_weighted).astype(jnp.bfloat16)
        db_ref[span(tb)] = (
            db_all[span(tb)] + dot(weighted_x[span(tb)], grad_end, NT)
        ).astype(jnp.bfloat16)
        product = d_weighted * x_ref[span(tb)].astype(jnp.float32)
        total = sums[span(tb)]
        for h in range(heads):
            total = total + jnp.where(
                lane == h + 8, jnp.sum(product[:, lanes(h)], axis=1, keepdims=True), 0.0
            )
        sums[span(tb)] = total
    turned = sums[...].T
    weight_sums = turned[8:16]
    reach_end = jnp.zeros((8, 1), jnp.float32)
    for h in range(heads):
        reach_end = reach_end + jnp.where(
            iota((8, 1), 0) == h, jnp.sum(crossing[:, lanes(h)], axis=1, keepdims=True), 0.0
        )
    d_last = jnp.sum(weight_sums, axis=1, keepdims=True) + through * reach_end
    d_cumulative = turned[0:8] - column_sums[...] - weight_sums
    d_cumulative = d_cumulative + jnp.where(iota(step.shape, 1) == tokens - 1, d_last, 0.0)
    onward = (iota(square, 0) >= iota(square, 1)).astype(jnp.float32)
    d_exponent = dot(d_cumulative, onward, NN, HIGH)
    d_step = (column_sums[...] + weight_sums) / step - rate_ref[...] * d_exponent
    dstep_ref[...] = d_step / (1.0 + jnp.exp(-pre))

    for distance in range(1, reach + 1):
        state_copy(distance).wait_send()
        grad_copy(distance).wait_send()


def on_device(
    ssd_input,
    gate_input,
    state_maps,
    step_raw,
    step_bias,
    decay_rate,
    skip_gain,
    norm_gain,
    out_weight,
    reward_head,
    traj_lengths,
    step_pairs,
):
    tokens, channels = ssd_input.shape
    heads = step_raw.shape[1]
    model_width = out_weight.shape[0]
    seq_count, tensor_count = lax.axis_size("seq"), lax.axis_size("tensor")
    chips = tensor_count // 2
    half = model_width // (2 * chips)
    pieces = 2
    piece = tokens // pieces
    steps = chips - 1
    reach = -(-(longest - 1) // tokens)
    bf16, f32 = jnp.bfloat16, jnp.float32

    def twice(value):
        return jnp.concatenate([value, value], axis=0)

    wide = jnp.concatenate(
        [norm_gain[None, :], jnp.repeat(skip_gain, channels // heads)[None, :]]
        + [jnp.zeros((6, channels), f32)],
        axis=0,
    )
    operands = (
        ssd_input,
        gate_input,
        state_maps[:, 0],
        state_maps[:, 1],
        twice(step_raw.T),
        twice(step_bias)[:, None],
        twice(decay_rate)[:, None],
        wide,
        out_weight,
        reward_head[None, :],
        traj_lengths[None, :],
        traj_lengths[:, None],
        step_pairs[None, :],
    )
    vmem = pl.BlockSpec(memory_space=pltpu.VMEM)
    in_specs = [vmem] * len(operands)
    in_specs[8] = pl.BlockSpec(memory_space=pl.ANY)
    rewards, dx, dz, db, dc, dstep = pl.pallas_call(
        layer_kernel,
        out_shape=(
            jax.ShapeDtypeStruct((8, tokens), f32),
            jax.ShapeDtypeStruct((tokens, channels), bf16),
            jax.ShapeDtypeStruct((tokens, channels), bf16),
            jax.ShapeDtypeStruct((tokens, STATE), bf16),
            jax.ShapeDtypeStruct((tokens, STATE), bf16),
            jax.ShapeDtypeStruct((8, tokens), f32),
        ),
        in_specs=in_specs,
        out_specs=(vmem,) * 6,
        scratch_shapes=[
            pltpu.VMEM((model_width, channels), bf16),
            pltpu.VMEM((tokens, BLOCK), f32),
            pltpu.VMEM((heads, tokens, tokens), f32),
            pltpu.VMEM((tokens, tokens), f32),
            pltpu.VMEM((tokens, channels), f32),
            pltpu.VMEM((tokens, channels), f32),
            pltpu.VMEM((STATE, channels), f32),
            pltpu.VMEM((tokens, channels), bf16),
            pltpu.VMEM((tokens, channels), bf16),
            pltpu.VMEM((tokens, BLOCK), f32),
            pltpu.VMEM((tokens, BLOCK), f32),
            pltpu.VMEM((STATE + 16, channels), bf16),
            pltpu.VMEM((reach, STATE + 16, channels), bf16),
            pltpu.VMEM((STATE + 16, channels), bf16),
            pltpu.VMEM((reach, STATE + 16, channels), bf16),
            pltpu.VMEM((tokens, channels), bf16),
            pltpu.VMEM((tokens, channels), bf16),
            pltpu.VMEM((tokens, channels), f32),
            pltpu.VMEM((tokens, STATE), f32),
            pltpu.VMEM((tokens, BLOCK), f32),
            pltpu.VMEM((8, tokens), f32),
            pltpu.VMEM((tokens, channels), f32),
            pltpu.VMEM((seq_count, 8, tokens), f32),
            pltpu.VMEM((2, pieces, piece, half), bf16),
            pltpu.VMEM((2, steps, pieces, piece, half), bf16),
            pltpu.VMEM((2, pieces, piece, half), bf16),
            pltpu.VMEM((2, pieces, piece, half), bf16),
            pltpu.VMEM((chips, 2, pieces, piece, half), bf16),
            pltpu.VMEM((8, tokens), f32),
            pltpu.VMEM((tensor_count, 8, tokens), f32),
            pltpu.VMEM((8, tokens), f32),
            pltpu.SemaphoreType.DMA,
            pltpu.SemaphoreType.DMA((reach,)),
            pltpu.SemaphoreType.DMA((reach,)),
            pltpu.SemaphoreType.DMA((reach,)),
            pltpu.SemaphoreType.DMA((reach,)),
            pltpu.SemaphoreType.DMA((2, steps, pieces)),
            pltpu.SemaphoreType.DMA((2, steps, pieces)),
            pltpu.SemaphoreType.DMA((2, pieces)),
            pltpu.SemaphoreType.DMA((2, pieces)),
            pltpu.SemaphoreType.DMA((2, steps, pieces)),
            pltpu.SemaphoreType.DMA((2, steps, pieces)),
            pltpu.SemaphoreType.DMA((tensor_count,)),
            pltpu.SemaphoreType.DMA((tensor_count,)),
            pltpu.SemaphoreType.DMA((seq_count,)),
            pltpu.SemaphoreType.DMA((seq_count,)),
        ],
        compiler_params=pltpu.CompilerParams(
            collective_id=0, has_side_effects=True, vmem_limit_bytes=48 << 20
        ),
        name="layer",
    )(*operands)
    return (rewards[0], dx, dz, jnp.stack([db, dc], axis=1), dstep[:heads].T)


def solution(mesh):
    return jax.shard_map(
        on_device,
        mesh=mesh,
        in_specs=(
            P("seq", "tensor"),
            P("seq", "tensor"),
            P("seq", None, "tensor"),
            P("seq", "tensor"),
            P("tensor"),
            P("tensor"),
            P("tensor"),
            P("tensor"),
            P(None, "tensor"),
            P(),
            P(),
            P(),
        ),
        out_specs=(
            P("seq"),
            P("seq", "tensor"),
            P("seq", "tensor"),
            P("seq", None, "tensor"),
            P("seq", "tensor"),
        ),
        check_vma=False,
    )
```

profile of v0, /device:TPU:15, one launch (start us, length us, event | category | flops | bytes accessed | tf_op | source)
XLA Modules:
  0.0 121.9 jit_solution(9775144450723429647)
XLA Ops:
  0.6 0.8 maximum_bitcast_fusion
  1.4 0.8 maximum_bitcast_fusion.1
  2.2 0.1 pad.4.clone
  2.3 0.7 broadcast_in_dim.30
  3.0 0.1 copy.20.rate_ref
  3.1 0.1 copy.19.bias_ref
  3.2 0.8 pad_maximum_fusion.1.raw_ref
  4.0 0.8 maximum_maximum_fusion.wide_ref
  4.7 0.7 copy.21.length_col_ref
  5.5 1.4 %fusion = (bf16[384,1,128]{2,1,0:T(2,128)(2,1)S(1)}, bf16[384,1,128]{2,1,0:T(2,128)(2,1)S(1)}) fusion(bf16[384,2,128]{2,1,0:T(2,128)(2,1)} %param.14), kind=kLoop, calls=%fused_computation.9 | loop fusion | bytes 393216 | tf_op jit(solution)/shard_map/slice | solution.py:690
  6.9 0.0 copy-start
  6.9 1.0 copy-done
  7.9 0.0 copy-start.1
  7.9 1.0 copy-done.1
  8.9 0.0 copy-start.2
  8.9 0.7 copy-done.2
  9.6 0.0 copy-start.3
  9.6 0.7 copy-done.3
  10.4 0.0 copy-start.4
  10.4 0.7 copy-done.4
  11.0 107.3 %layer.1 = (f32[8,384]{1,0:T(8,128)S(1)}, bf16[384,512]{1,0:T(8,128)(2,1)S(1)}, bf16[384,512]{1,0:T(8,128)(2,1)S(1)}, bf16[384,128]{1,0:T(8,128)(2,1)S(1)}, bf16...) custom-call(bf16[384,512]{1,0:T(8,128)(2,1)S(1)} %copy-done, bf16[384,512]{1,0:T(8,128)(2,1)S(1)} %copy-done.1, ...), custom_call_target="tpu_custom_call" | custom-call | tf_op jit(solution)/shard_map/layer/pallas_call | solution.py:704
  118.3 0.6 slice_reduce_fusion
  118.9 0.6 slice_bitcast_fusion
  119.6 0.9 copy.22
  120.4 0.7 copy.29
  121.2 0.7 copy.30
  (3 shorter events, 0.1 us)
Async XLA Ops:
  6.9 1.0 copy-start
  7.9 1.0 copy-start.1
  8.9 0.7 copy-start.2
  9.6 0.7 copy-start.3
  10.4 0.7 copy-start.4
where the time goes:
time: 122 us
  Pallas kernels  107 us (88%)
  local copies, waits for them, and re-layouts  10.8 us (9%)
  other arithmetic  3.16 us (3%)
    pallas_call x1, Pallas kernels, on_device(): pl.pallas_call(layer_kernel, out_shape=(jax.ShapeDtypeStruct((8, tokens),...  107 us
    unnamed x13, local copies, waits for them, and re-layouts  6.47 us

commit v1 on v0

--- a/solution.py
+++ b/solution.py
@@ -29,26 +29,35 @@
 
 
 def layer_kernel(
-    x_ref,
-    z_ref,
-    b_ref,
-    c_ref,
-    raw_ref,
+    x_hbm,
+    z_hbm,
+    maps_hbm,
+    raw_hbm,
     bias_ref,
     rate_ref,
-    wide_ref,
-    weight_ref,
-    head_ref,
-    length_row_ref,
-    length_col_ref,
-    pairs_ref,
+    skip_ref,
+    gain_hbm,
+    weight_hbm,
+    head_hbm,
+    length_hbm,
+    pairs_hbm,
     reward_out,
     dx_ref,
     dz_ref,
-    db_ref,
-    dc_ref,
+    dmaps_ref,
     dstep_ref,
     weight,
+    x_ref,
+    z_ref,
+    maps_ref,
+    raw_ref,
+    gain_ref,
+    head_ref,
+    length_ref,
+    pairs_ref,
+    maps_wide,
+    b_ref,
+    c_ref,
     columns,
     decays,
     scores,
@@ -71,25 +80,38 @@
     column_sums,
     back,
     rewards,
-    first,
-    moving,
+    late_out,
+    late_moving,
     swap_out,
     swap_in,
-    hidden,
+    late_hidden,
+    early_out,
+    early_moving,
+    halve_out,
+    halve_in,
+    early_hidden,
     own_stats,
     far_stats,
     own_reward,
-    weight_sem,
+    load_sems,
     state_send,
     state_recv,
     grad_send,
     grad_recv,
-    reduce_send,
-    reduce_recv,
+    late_reduce_send,
+    late_reduce_recv,
     swap_send,
     swap_recv,
-    gather_send,
-    gather_recv,
+    late_gather_send,
+    late_gather_recv,
+    early_reduce_send,
+    early_reduce_recv,
+    early_gather_send,
+    early_gather_recv,
+    halve_send,
+    halve_recv,
+    join_send,
+    join_recv,
     stats_send,
     stats_recv,
     reward_send,
@@ -106,17 +128,33 @@
     ways = (up, down)
     tokens, channels = x_ref.shape
     model_width = weight.shape[0]
-    half = hidden.shape[-1]
-    pieces = hidden.shape[2]
-    piece = tokens // pieces
-    width = channels // (raw_ref.shape[0] // 2)
+    late_pieces, piece, late_width = late_hidden.shape[2:]
+    early_pieces, _, early_width = early_hidden.shape[3:]
+    cut = late_pieces * piece
+    width = channels // (raw_ref.shape[0])
     heads = channels // width
     blocks = tokens // BLOCK
     reach = state_far.shape[0]
     pair_tiles = pairs_ref.shape[1] // BLOCK
 
-    weight_copy = pltpu.make_async_copy(weight_ref, weight, weight_sem)
-    weight_copy.start()
+    loads = [
+        pltpu.make_async_copy(source, target, load_sems.at[k])
+        for k, (source, target) in enumerate(
+            [
+                (raw_hbm, raw_ref),
+                (length_hbm, length_ref),
+                (maps_hbm, maps_ref),
+                (x_hbm, x_ref),
+                (pairs_hbm, pairs_ref),
+                (head_hbm, head_ref),
+                (gain_hbm, gain_ref),
+                (z_hbm, z_ref),
+                (weight_hbm, weight),
+            ]
+        )
+    ]
+    for load in loads:
+        load.start()
     barrier = pltpu.get_barrier_semaphore()
 
     def greet_tensor(k, _):
@@ -138,17 +176,24 @@
     def lanes(h):
         return slice(h * width, (h + 1) * width)
 
-    pre = raw_ref[...] + bias_ref[...]
+    def per_head(ref):
+        row = lax.rem(iota((8, 1), 0), heads)
+        return sum(jnp.where(row == h, ref[h], 0.0) for h in range(heads))
+
+    bias, rate = per_head(bias_ref), per_head(rate_ref)
+    for load in loads[:2]:
+        load.wait()
+    pre = jnp.concatenate([raw_ref[...], raw_ref[...]], axis=0) + bias
     step = jnp.maximum(pre, 0.0) + jnp.log1p(jnp.exp(-jnp.abs(pre)))
-    exponent = -step * rate_ref[...]
+    exponent = -step * rate
     square = (tokens, tokens)
     upto = (iota(square, 0) <= iota(square, 1)).astype(jnp.float32)
     cumulative = dot(exponent, upto, NN, HIGH)
-    count = length_row_ref.shape[1]
+    count = length_ref.shape[1]
     openings = jnp.sum(
         jnp.where(
             iota((count, count), 1) < iota((count, count), 0),
-            length_row_ref[...].astype(jnp.float32),
+            length_ref[...].astype(jnp.float32),
             0.0,
         ),
         axis=1,
@@ -234,6 +279,11 @@
                 carry = carry * passed
         return total
 
+    loads[2].wait()
+    maps_wide[...] = maps_ref[...].astype(jnp.float32)
+    b_ref[...] = maps_wide[pl.ds(0, tokens, stride=2), :].astype(jnp.bfloat16)
+    c_ref[...] = maps_wide[pl.ds(1, tokens, stride=2), :].astype(jnp.bfloat16)
+    loads[3].wait()
     for tb in range(blocks):
         weighted_x[span(tb)] = (
             x_ref[span(tb)].astype(jnp.float32) * expanded(0, tb)
@@ -260,6 +310,8 @@
                 (decay * score).astype(jnp.bfloat16), x_ref[0:reached, lanes(h)], NN
             )
 
+    for load in loads[4:8]:
+        load.wait()
     reward_row = head_ref[...]
     high = reward_row.astype(jnp.bfloat16).astype(jnp.float32)
     rest = reward_row - high
@@ -270,7 +322,7 @@
         high,
         jnp.where(term == 1, middle, jnp.where(term == 2, rest - middle, 0.0)),
     ).astype(jnp.bfloat16)
-    weight_copy.wait()
+    loads[8].wait()
     reward_channels = jnp.sum(dot(terms, weight[...], NN), axis=0, keepdims=True)
 
     tile = (BLOCK, BLOCK)
@@ -311,7 +363,8 @@
         state_copy(distance).wait_recv()
     state_in[...] = gathered(state_far)
     incoming = state_in[...].astype(jnp.bfloat16)
-    gain, skip = wide_ref[0:1], wide_ref[1:2]
+    gain = gain_ref[...]
+    skip = jnp.concatenate([jnp.full((1, width), skip_ref[h]) for h in range(heads)], axis=1)
 
     def gating(tb):
         y = y_all[span(tb)]
@@ -331,140 +384,245 @@
         _, _, _, _, gated, inverse = gating(tb)
         mixed[span(tb)] = (gated * inverse * gain).astype(jnp.bfloat16)
 
+    last = chips - 2
+
     def chunk(way, distance):
-        move = distance if way == 1 else chips - distance
-        return lax.rem(place + move, chips)
-
-    def rows(index, way):
-        return pl.ds(pl.multiple_of((index * 2 + way) * half, half), half)
-
-    def own_part(way, distance):
-        return lax.dot_general(
-            mixed[...],
-            weight[rows(chunk(way, distance), way), :],
-            (((1,), (1,)), ((), ())),
-            preferred_element_type=jnp.float32,
-        )
-
-    def reduce_copy(way, step, j, source):
+        return lax.rem(place + chips + (distance if way == 0 else -distance), chips)
+
+    def part_half(way, i):
+        odd = lax.rem(i, 2)
+        return odd if way == 0 else 1 - odd
+
+    def reduce_spot(way, i):
+        return chunk(way, chips // 2 - lax.div(i + 1, 2)), part_half(way, i)
+
+    def gather_spot(way, i):
+        return chunk(way, -lax.div(i, 2)), part_half(way, i)
+
+    def late_rows(spot):
+        index, part = spot
+        return pl.ds(pl.multiple_of((index * 2 + part) * late_width, late_width), late_width)
+
+    def early_rows(spot, owner):
+        index, part = spot
+        start = ((index * 2 + owner) * 2 + part) * early_width
+        return pl.ds(pl.multiple_of(start, early_width), early_width)
+
+    def late_part(spot):
+        return dot(mixed[0:cut], weight[late_rows(spot), :], NT)
+
+    def early_part(spot, owner):
+        return dot(mixed[cut:], weight[early_rows(spot, owner), :], NT)
+
+    def remote(source, target, send, recv, device):
         return pltpu.make_async_remote_copy(
             src_ref=source,
-            dst_ref=moving.at[way, step, j],
-            send_sem=reduce_send.at[way, step, j],
-            recv_sem=reduce_recv.at[way, step, j],
-            device_id=ways[way],
+            dst_ref=target,
+            send_sem=send,
+            recv_sem=recv,
+            device_id=device,
             device_id_type=MESH,
         )
 
-    def reduce_source(way, step, j):
-        return first.at[way, j] if step is None else moving.at[way, step, j]
-
-    for way in range(2):
-        part = own_part(way, 1)
-        for j in range(pieces):
-            first[way, j] = part[j * piece : (j + 1) * piece].astype(jnp.bfloat16)
-    for j in range(pieces):
+    def late_reduce(way, i, j):
+        return remote(
+            late_out.at[way, i, j],
+            late_moving.at[way, i, j],
+            late_reduce_send.at[way, i, j],
+            late_reduce_recv.at[way, i, j],
+            ways[way],
+        )
+
+    def early_reduce(way, i, j):
+        return remote(
+            early_out.at[way, i, j],
+            early_moving.at[way, i, j],
+            early_reduce_send.at[way, i, j],
+            early_reduce_recv.at[way, i, j],
+            ways[way],
+        )
+
+    def halve_copy(way, i, j):
+        return remote(
+            halve_out.at[way, i, j],
+            halve_in.at[way, i, j],
+            halve_send.at[way, i, j],
+            halve_recv.at[way, i, j],
+            across,
+        )
+
+    def swap_copy(way, j):
+        return remote(
+            swap_out.at[way, j], swap_in.at[way, j], swap_send.at[way, j], swap_recv.at[way, j], across
+        )
+
+    def late_gather(way, i, j):
+        index, part = gather_spot(way, i)
+        spot = late_hidden.at[index, part, j]
+        return remote(
+            spot, spot, late_gather_send.at[way, i, j], late_gather_recv.at[way, i, j], ways[way]
+        )
+
+    def early_gather(way, i, j):
+        index, part = gather_spot(way, i)
+        spot = early_hidden.at[index, side, part, j]
+        return remote(
+            spot, spot, early_gather_send.at[way, i, j], early_gather_recv.at[way, i, j], ways[way]
+        )
+
+    def arrived_spot(way, i):
+        return chunk(way, -lax.div(i, 2) - 1), part_half(way, i)
+
+    def join_copy(way, i, j, at):
+        index, part = at
+        spot = early_hidden.at[index, side, part, j]
+        return remote(spot, spot, join_send.at[way, i, j], join_recv.at[way, i, j], across)
+
+    late_turns = [(j, way) for j in range(late_pieces) for way in range(2)]
+    early_turns = [(j, way) for j in range(early_pieces) for way in range(2)]
+
+    def cut_piece(value, j):
+        return value[j * piece : (j + 1) * piece]
+
+    def start_halving(i, at=None):
         for way in range(2):
-            reduce_copy(way, 0, j, first.at[way, j]).start()
-
-    along = lax.dot_general(
-        jnp.broadcast_to(reward_channels, (8, channels)),
-        mixed[...].astype(jnp.float32),
-        (((1,), (1,)), ((), ())),
-        preferred_element_type=jnp.float32,
-        precision=lax.Precision.HIGHEST,
-    )
-
-    def reduce_step(step, _):
-        parts = [own_part(way, step + 2) for way in range(2)]
-        for j in range(pieces):
-            for way in range(2):
-                reduce_copy(way, step, j, moving.at[way, step, j]).wait_recv()
-                moving[way, step, j] = (
-                    moving[way, step, j].astype(jnp.float32)
-                    + parts[way][j * piece : (j + 1) * piece]
-                ).astype(jnp.bfloat16)
-                reduce_copy(way, step + 1, j, moving.at[way, step, j]).start()
+            part = early_part(reduce_spot(way, i) if at is None else at[way], 1 - side)
+            for j in range(early_pieces):
+                halve_out[way, i, j] = cut_piece(part, j).astype(jnp.bfloat16)
+                halve_copy(way, i, j).start()
+
+    def start_late(i):
+        for way in range(2):
+            part = late_part(reduce_spot(way, i))
+            for j in range(late_pieces):
+                late_out[way, i, j] = cut_piece(part, j).astype(jnp.bfloat16)
+                late_reduce(way, i, j).start()
+
+    def start_early(i):
+        parts = [early_part(reduce_spot(way, i), side) for way in range(2)]
+        for j, way in early_turns:
+            halve_copy(way, i, j).wait_recv()
+            early_out[way, i, j] = (
+                cut_piece(parts[way], j) + halve_in[way, i, j].astype(jnp.float32)
+            ).astype(jnp.bfloat16)
+            early_reduce(way, i, j).start()
+
+    start_halving(0)
+    start_late(0)
+    start_halving(1)
+    start_late(1)
+    start_halving(2)
+    start_early(0)
+    start_halving(3)
+    start_early(1)
+
+    along = dot(
+        jnp.broadcast_to(reward_channels, (8, channels)), mixed[...].astype(jnp.float32), NT, HIGH
+    )
+
+    own_spots = [(place, way) for way in range(2)]
+
+    def reduce_work(i):
+        late_parts = [late_part(reduce_spot(way, i + 2)) for way in range(2)]
+        early_parts = [early_part(reduce_spot(way, i + 2), side) for way in range(2)]
+
+        def late_turn(j, way):
+            late_reduce(way, i, j).wait_recv()
+            late_out[way, i + 2, j] = (
+                late_moving[way, i, j].astype(jnp.float32) + cut_piece(late_parts[way], j)
+            ).astype(jnp.bfloat16)
+            late_reduce(way, i + 2, j).start()
+
+        def early_turn(j, way):
+            halve_copy(way, i + 2, j).wait_recv()
+            early_reduce(way, i, j).wait_recv()
+            early_out[way, i + 2, j] = (
+                early_moving[way, i, j].astype(jnp.float32)
+                + cut_piece(early_parts[way], j)
+                + halve_in[way, i + 2, j].astype(jnp.float32)
+            ).astype(jnp.bfloat16)
+            early_reduce(way, i + 2, j).start()
+
+        for k in range(max(len(late_turns), len(early_turns))):
+            if k < len(late_turns):
+                late_turn(*late_turns[k])
+            if k < len(early_turns):
+                early_turn(*early_turns[k])
+
+    def reduce_step(i, _):
+        start_halving(i + 4)
+        reduce_work(i)
         return 0
 
-    lax.fori_loop(0, chips - 2, reduce_step, 0)
-
-    def swap_copy(way, j):
-        return pltpu.make_async_remote_copy(
-            src_ref=swap_out.at[way, j],
-            dst_ref=swap_in.at[way, j],
-            send_sem=swap_send.at[way, j],
-            recv_sem=swap_recv.at[way, j],
-            device_id=across,
-            device_id_type=MESH,
-        )
-
-    last = chips - 2
-    parts = [own_part(way, chips) for way in range(2)]
-    for j in range(pieces):
-        for way in range(2):
-            reduce_copy(way, last, j, moving.at[way, last, j]).wait_recv()
-            swap_out[way, j] = (
-                moving[way, last, j].astype(jnp.float32) + parts[way][j * piece : (j + 1) * piece]
-            ).astype(jnp.bfloat16)
-            swap_copy(way, j).start()
-
-    def gather_copy(way, step, j):
-        index = chunk(way, chips + step if way == 1 else step)
-        return pltpu.make_async_remote_copy(
-            src_ref=hidden.at[index, way, j],
-            dst_ref=hidden.at[index, way, j],
-            send_sem=gather_send.at[way, step, j],
-            recv_sem=gather_recv.at[way, step, j],
-            device_id=ways[way],
-            device_id_type=MESH,
-        )
-
-    for j in range(pieces):
-        for way in range(2):
-            swap_copy(way, j).wait_recv()
-            hidden[place, way, j] = (
-                swap_out[way, j].astype(jnp.float32) + swap_in[way, j].astype(jnp.float32)
-            ).astype(jnp.bfloat16)
-            gather_copy(way, 0, j).start()
-
-    ones = jnp.ones((8, half), jnp.float32)
-    squares = []
-    for j in range(pieces):
+    lax.fori_loop(0, last - 3, reduce_step, 0)
+    start_halving(last + 1, own_spots)
+    lax.fori_loop(last - 3, last - 1, lambda i, _: reduce_work(i) or 0, 0)
+
+    late_parts = [late_part(own_spots[way]) for way in range(2)]
+    early_parts = [early_part(own_spots[way], side) for way in range(2)]
+    for j, way in late_turns:
+        late_reduce(1 - way, last - 1, j).wait_recv()
+        late_reduce(way, last, j).wait_recv()
+        swap_out[way, j] = (
+            late_moving[way, last, j].astype(jnp.float32)
+            + late_moving[1 - way, last - 1, j].astype(jnp.float32)
+            + cut_piece(late_parts[way], j)
+        ).astype(jnp.bfloat16)
+        swap_copy(way, j).start()
+    for j, way in early_turns:
+        halve_copy(way, last + 1, j).wait_recv()
+        early_reduce(1 - way, last - 1, j).wait_recv()
+        early_reduce(way, last, j).wait_recv()
+        early_hidden[place, side, way, j] = (
+            early_moving[way, last, j].astype(jnp.float32)
+            + early_moving[1 - way, last - 1, j].astype(jnp.float32)
+            + cut_piece(early_parts[way], j)
+            + halve_in[way, last + 1, j].astype(jnp.float32)
+        ).astype(jnp.bfloat16)
+        early_gather(way, 0, j).start()
+        early_gather(1 - way, 1, j).start()
+    for j, way in late_turns:
+        swap_copy(way, j).wait_recv()
+        late_hidden[place, way, j] = (
+            swap_out[way, j].astype(jnp.float32) + swap_in[way, j].astype(jnp.float32)
+        ).astype(jnp.bfloat16)
+        late_gather(way, 0, j).start()
+        late_gather(1 - way, 1, j).start()
+    for j, way in early_turns:
+        join_copy(way, 0, j, own_spots[way]).start()
+
+    def squares(read, columns_count):
         total = None
         for way in range(2):
-            value = hidden[place, way, j].astype(jnp.float32)
+            value = read(way).astype(jnp.float32)
             total = value * value if total is None else total + value * value
-        squares.append(
-            lax.dot_general(
-                ones,
-                total,
-                (((1,), (1,)), ((), ())),
-                preferred_element_type=jnp.float32,
-                precision=lax.Precision.HIGHEST,
-            )
-        )
-    is_along = lax.broadcasted_iota(jnp.int32, (8, tokens), 0) == 0
-    own_stats[...] = jnp.where(is_along, along, 0.5 * jnp.concatenate(squares, axis=1))
+        return dot(jnp.ones((8, columns_count), jnp.float32), total, NT, HIGH)
+
+    late_squares = squares(lambda way: late_hidden[place, way].reshape(cut, late_width), late_width)
+    early_squares = squares(
+        lambda way: early_hidden[place, side, way].reshape(tokens - cut, early_width), early_width
+    )
+    is_along = iota((8, tokens), 0) == 0
+    own_stats[...] = jnp.where(
+        is_along, along, jnp.concatenate([0.5 * late_squares, early_squares], axis=1)
+    )
 
     def stats_copy(k):
-        return pltpu.make_async_remote_copy(
-            src_ref=own_stats,
-            dst_ref=far_stats.at[k],
-            send_sem=stats_send.at[k],
-            recv_sem=stats_recv.at[k],
-            device_id=(seq, lax.rem(tensor + k, tensor_count)),
-            device_id_type=MESH,
+        return remote(
+            own_stats,
+            far_stats.at[k],
+            stats_send.at[k],
+            stats_recv.at[k],
+            (seq, lax.rem(tensor + k, tensor_count)),
         )
 
     def reward_copy(k):
-        return pltpu.make_async_remote_copy(
-            src_ref=own_reward,
-            dst_ref=rewards.at[seq],
-            send_sem=reward_send.at[k],
-            recv_sem=reward_recv.at[k],
-            device_id=(lax.rem(seq + k, seq_count), tensor),
-            device_id_type=MESH,
+        return remote(
+            own_reward,
+            rewards.at[seq],
+            reward_send.at[k],
+            reward_recv.at[k],
+            (lax.rem(seq + k, seq_count), tensor),
         )
 
     def start_stats(k, _):
@@ -473,25 +631,51 @@
 
     lax.fori_loop(1, tensor_count, start_stats, 0)
 
-    def back_part(index, way):
-        return lax.dot_general(
-            hidden[index, way].reshape(tokens, half),
-            weight[rows(index, way), :],
-            (((1,), (0,)), ((), ())),
-            preferred_element_type=jnp.float32,
-        )
-
-    back[...] = back_part(place, 0) + back_part(place, 1)
-
-    def gather_step(step, _):
-        for j in range(pieces):
-            for way in range(2):
-                gather_copy(way, step, j).wait_recv()
-                gather_copy(way, step + 1, j).start()
-        back[...] += back_part(chunk(0, step + 1), 0) + back_part(chunk(1, step + 1), 1)
+    def late_back(spot):
+        index, part = spot
+        return dot(late_hidden[index, part].reshape(cut, late_width), weight[late_rows(spot), :], NN)
+
+    def early_back(spot, owner):
+        index, part = spot
+        return dot(
+            early_hidden[index, owner, part].reshape(tokens - cut, early_width),
+            weight[early_rows(spot, owner), :],
+            NN,
+        )
+
+    def add_joined(i, spots):
+        for j, way in early_turns:
+            join_copy(way, i, j, spots[way]).wait_recv()
+        back[cut:] += early_back(spots[0], 1 - side) + early_back(spots[1], 1 - side)
+
+    back[0:cut] = late_back(own_spots[0]) + late_back(own_spots[1])
+    back[cut:] = early_back(own_spots[0], side) + early_back(own_spots[1], side)
+
+    def take(i, forward):
+        spots = [arrived_spot(way, i) for way in range(2)]
+        for k in range(max(len(late_turns), len(early_turns))):
+            if k < len(early_turns):
+                j, way = early_turns[k]
+                early_gather(way, i, j).wait_recv()
+                if forward:
+                    early_gather(way, i + 2, j).start()
+                join_copy(way, i + 1, j, spots[way]).start()
+            if k < len(late_turns):
+                j, way = late_turns[k]
+                late_gather(way, i, j).wait_recv()
+                if forward:
+                    late_gather(way, i + 2, j).start()
+        back[0:cut] += late_back(spots[0]) + late_back(spots[1])
+        back[cut:] += early_back(spots[0], side) + early_back(spots[1], side)
+
+    def gather_step(i, _):
+        take(i, True)
+        add_joined(i, [arrived_spot(way, i - 1) for way in range(2)])
         return 0
 
-    lax.fori_loop(0, 2, gather_step, 0)
+    take(0, True)
+    add_joined(0, own_spots)
+    gather_step(1, 0)
 
     def add_stats(k, total):
         stats_copy(k).wait_recv()
@@ -507,11 +691,11 @@
         return 0
 
     lax.fori_loop(1, seq_count, start_reward, 0)
-    lax.fori_loop(2, chips - 2, gather_step, 0)
-    for j in range(pieces):
-        for way in range(2):
-            gather_copy(way, last, j).wait_recv()
-    back[...] += back_part(chunk(0, chips - 1), 0) + back_part(chunk(1, chips - 1), 1)
+    lax.fori_loop(2, last - 1, gather_step, 0)
+    for i in (last - 1, last):
+        take(i, False)
+        add_joined(i, [arrived_spot(way, i - 1) for way in range(2)])
+    add_joined(last + 1, [arrived_spot(way, last) for way in range(2)])
 
     def end_reward(k, _):
         reward_copy(k).wait()
@@ -519,25 +703,7 @@
 
     lax.fori_loop(1, seq_count, end_reward, 0)
 
-    def end_stats(k, _):
-        stats_copy(k).wait_send()
-        return 0
-
-    lax.fori_loop(1, tensor_count, end_stats, 0)
-
-    def end_ring(step, _):
-        for j in range(pieces):
-            for way in range(2):
-                reduce_copy(way, step, j, first.at[way, j]).wait_send()
-                gather_copy(way, step, j).wait_send()
-        return 0
-
-    lax.fori_loop(0, chips - 1, end_ring, 0)
-    for j in range(pieces):
-        for way in range(2):
-            swap_copy(way, j).wait_send()
-
-    reward_out[...] = own_reward[...]
+    reward_out[...] = own_reward[0:1]
 
     facts = jnp.concatenate(
         [stats, jnp.broadcast_to(scale, stats.shape), own_reward[...]]
@@ -606,9 +772,9 @@
             dx_all[0:reached, lanes(h)] += dot((decay * score).astype(jnp.bfloat16), dy, TN)
         sums[span(tb)] = row_sums
         d_score = d_score.astype(jnp.bfloat16)
-        dc_ref[span(tb)] = (
-            dot(d_score, b_ref[0:reached], NN) + dot(faded_dy[span(tb)], incoming, NT)
-        ).astype(jnp.bfloat16)
+        maps_wide[pl.ds(2 * tb * BLOCK + 1, BLOCK, stride=2), :] = dot(
+            d_score, b_ref[0:reached], NN
+        ) + dot(faded_dy[span(tb)], incoming, NT)
         db_all[0:reached] += dot(d_score, c_ref[span(tb)], TN)
 
     for distance in range(1, reach + 1):
@@ -619,9 +785,9 @@
     for tb in range(blocks):
         d_weighted = expanded(0, tb) * dot(b_ref[span(tb)], grad_end, NN)
         dx_ref[span(tb)] = (dx_all[span(tb)] + d_weighted).astype(jnp.bfloat16)
-        db_ref[span(tb)] = (
-            db_all[span(tb)] + dot(weighted_x[span(tb)], grad_end, NT)
-        ).astype(jnp.bfloat16)
+        maps_wide[pl.ds(2 * tb * BLOCK, BLOCK, stride=2), :] = db_all[span(tb)] + dot(
+            weighted_x[span(tb)], grad_end, NT
+        )
         product = d_weighted * x_ref[span(tb)].astype(jnp.float32)
         total = sums[span(tb)]
         for h in range(heads):
@@ -629,6 +795,7 @@
                 lane == h + 8, jnp.sum(product[:, lanes(h)], axis=1, keepdims=True), 0.0
             )
         sums[span(tb)] = total
+    dmaps_ref[...] = maps_wide[...].astype(jnp.bfloat16)
     turned = sums[...].T
     weight_sums = turned[8:16]
     reach_end = jnp.zeros((8, 1), jnp.float32)
@@ -641,12 +808,56 @@
     d_cumulative = d_cumulative + jnp.where(iota(step.shape, 1) == tokens - 1, d_last, 0.0)
     onward = (iota(square, 0) >= iota(square, 1)).astype(jnp.float32)
     d_exponent = dot(d_cumulative, onward, NN, HIGH)
-    d_step = (column_sums[...] + weight_sums) / step - rate_ref[...] * d_exponent
-    dstep_ref[...] = d_step / (1.0 + jnp.exp(-pre))
+    d_step = (column_sums[...] + weight_sums) / step - rate * d_exponent
+    dstep_ref[...] = (d_step / (1.0 + jnp.exp(-pre)))[0:heads]
 
     for distance in range(1, reach + 1):
         state_copy(distance).wait_send()
         grad_copy(distance).wait_send()
+
+    def end_stats(k, _):
+        stats_copy(k).wait_send()
+        return 0
+
+    lax.fori_loop(1, tensor_count, end_stats, 0)
+
+    def end_ring(step, _):
+        for j, way in late_turns:
+            late_reduce(way, step, j).wait_send()
+            late_gather(way, step, j).wait_send()
+        for j, way in early_turns:
+            early_reduce(way, step, j).wait_send()
+            early_gather(way, step, j).wait_send()
+        return 0
+
+    def end_side(step, _):
+        for j, way in early_turns:
+            halve_copy(way, step, j).wait_send()
+            join_copy(way, step, j, own_spots[way]).wait_send()
+        return 0
+
+    lax.fori_loop(0, chips - 1, end_ring, 0)
+    lax.fori_loop(0, chips, end_side, 0)
+    for j, way in late_turns:
+        swap_copy(way, j).wait_send()
+
+
+def deliver_kernel(*refs):
+    count = len(refs) // 2
+    for source, target in zip(refs[:count], refs[count:]):
+        target[...] = source[...]
+
+
+def deliver(values):
+    vmem = pl.BlockSpec(memory_space=pltpu.VMEM)
+    return pl.pallas_call(
+        deliver_kernel,
+        out_shape=tuple(jax.ShapeDtypeStruct(v.shape, v.dtype) for v in values),
+        in_specs=[vmem] * len(values),
+        out_specs=(vmem,) * len(values),
+        compiler_params=pltpu.CompilerParams(vmem_limit_bytes=60 << 20),
+        name="deliver",
+    )(*values)
 
 
 def on_device(
@@ -668,53 +879,55 @@
     model_width = out_weight.shape[0]
     seq_count, tensor_count = lax.axis_size("seq"), lax.axis_size("tensor")
     chips = tensor_count // 2
-    half = model_width // (2 * chips)
-    pieces = 2
-    piece = tokens // pieces
+    late_width = model_width // (2 * chips)
+    early_width = late_width // 2
+    late_pieces, early_pieces = 1, 1
+    piece = tokens // (late_pieces + early_pieces)
     steps = chips - 1
     reach = -(-(longest - 1) // tokens)
     bf16, f32 = jnp.bfloat16, jnp.float32
 
-    def twice(value):
-        return jnp.concatenate([value, value], axis=0)
-
-    wide = jnp.concatenate(
-        [norm_gain[None, :], jnp.repeat(skip_gain, channels // heads)[None, :]]
-        + [jnp.zeros((6, channels), f32)],
-        axis=0,
-    )
     operands = (
         ssd_input,
         gate_input,
-        state_maps[:, 0],
-        state_maps[:, 1],
-        twice(step_raw.T),
-        twice(step_bias)[:, None],
-        twice(decay_rate)[:, None],
-        wide,
+        state_maps.reshape(2 * tokens, STATE),
+        step_raw.T,
+        step_bias,
+        decay_rate,
+        skip_gain,
+        norm_gain[None, :],
         out_weight,
         reward_head[None, :],
         traj_lengths[None, :],
-        traj_lengths[:, None],
         step_pairs[None, :],
     )
     vmem = pl.BlockSpec(memory_space=pltpu.VMEM)
-    in_specs = [vmem] * len(operands)
-    in_specs[8] = pl.BlockSpec(memory_space=pl.ANY)
-    rewards, dx, dz, db, dc, dstep = pl.pallas_call(
+    hbm = pl.BlockSpec(memory_space=pltpu.HBM)
+    smem = pl.BlockSpec(memory_space=pltpu.SMEM)
+    results = pl.pallas_call(
         layer_kernel,
         out_shape=(
-            jax.ShapeDtypeStruct((8, tokens), f32),
+            jax.ShapeDtypeStruct((1, tokens), f32),
             jax.ShapeDtypeStruct((tokens, channels), bf16),
             jax.ShapeDtypeStruct((tokens, channels), bf16),
-            jax.ShapeDtypeStruct((tokens, STATE), bf16),
-            jax.ShapeDtypeStruct((tokens, STATE), bf16),
-            jax.ShapeDtypeStruct((8, tokens), f32),
+            jax.ShapeDtypeStruct((2 * tokens, STATE), bf16),
+            jax.ShapeDtypeStruct((heads, tokens), f32),
         ),
-        in_specs=in_specs,
-        out_specs=(vmem,) * 6,
+        in_specs=[hbm] * 4 + [smem] * 3 + [hbm] * 5,
+        out_specs=(vmem,) * 5,
         scratch_shapes=[
             pltpu.VMEM((model_width, channels), bf16),
+            pltpu.VMEM((tokens, channels), bf16),
+            pltpu.VMEM((tokens, channels), bf16),
+            pltpu.VMEM((2 * tokens, STATE), bf16),
+            pltpu.VMEM((heads, tokens), f32),
+            pltpu.VMEM((1, channels), f32),
+            pltpu.VMEM((1, model_width), f32),
+            pltpu.VMEM((1, traj_lengths.shape[0]), jnp.int32),
+            pltpu.VMEM((1, step_pairs.shape[0]), jnp.int32),
+            pltpu.VMEM((2 * tokens, STATE), f32),
+            pltpu.VMEM((tokens, STATE), bf16),
+            pltpu.VMEM((tokens, STATE), bf16),
             pltpu.VMEM((tokens, BLOCK), f32),
             pltpu.VMEM((heads, tokens, tokens), f32),
             pltpu.VMEM((tokens, tokens), f32),
@@ -737,36 +950,56 @@
             pltpu.VMEM((8, tokens), f32),
             pltpu.VMEM((tokens, channels), f32),
             pltpu.VMEM((seq_count, 8, tokens), f32),
-            pltpu.VMEM((2, pieces, piece, half), bf16),
-            pltpu.VMEM((2, steps, pieces, piece, half), bf16),
-            pltpu.VMEM((2, pieces, piece, half), bf16),
-            pltpu.VMEM((2, pieces, piece, half), bf16),
-            pltpu.VMEM((chips, 2, pieces, piece, half), bf16),
+            pltpu.VMEM((2, steps, late_pieces, piece, late_width), bf16),
+            pltpu.VMEM((2, steps, late_pieces, piece, late_width), bf16),
+            pltpu.VMEM((2, late_pieces, piece, late_width), bf16),
+            pltpu.VMEM((2, late_pieces, piece, late_width), bf16),
+            pltpu.VMEM((chips, 2, late_pieces, piece, late_width), bf16),
+            pltpu.VMEM((2, steps, early_pieces, piece, early_width), bf16),
+            pltpu.VMEM((2, steps, early_pieces, piece, early_width), bf16),
+            pltpu.VMEM((2, chips, early_pieces, piece, early_width), bf16),
+            pltpu.VMEM((2, chips, early_pieces, piece, early_width), bf16),
+            pltpu.VMEM((chips, 2, 2, early_pieces, piece, early_width), bf16),
             pltpu.VMEM((8, tokens), f32),
             pltpu.VMEM((tensor_count, 8, tokens), f32),
             pltpu.VMEM((8, tokens), f32),
-            pltpu.SemaphoreType.DMA,
+            pltpu.SemaphoreType.DMA((9,)),
             pltpu.SemaphoreType.DMA((reach,)),
             pltpu.SemaphoreType.DMA((reach,)),
             pltpu.SemaphoreType.DMA((reach,)),
             pltpu.SemaphoreType.DMA((reach,)),
-            pltpu.SemaphoreType.DMA((2, steps, pieces)),
-            pltpu.SemaphoreType.DMA((2, steps, pieces)),
-            pltpu.SemaphoreType.DMA((2, pieces)),
-            pltpu.SemaphoreType.DMA((2, pieces)),
-            pltpu.SemaphoreType.DMA((2, steps, pieces)),
-            pltpu.SemaphoreType.DMA((2, steps, pieces)),
+            pltpu.SemaphoreType.DMA((2, steps, late_pieces)),
+            pltpu.SemaphoreType.DMA((2, steps, late_pieces)),
+            pltpu.SemaphoreType.DMA((2, late_pieces)),
+            pltpu.SemaphoreType.DMA((2, late_pieces)),
+            pltpu.SemaphoreType.DMA((2, steps, late_pieces)),
+            pltpu.SemaphoreType.DMA((2, steps, late_pieces)),
+            pltpu.SemaphoreType.DMA((2, steps, early_pieces)),
+            pltpu.SemaphoreType.DMA((2, steps, early_pieces)),
+            pltpu.SemaphoreType.DMA((2, steps, early_pieces)),
+            pltpu.SemaphoreType.DMA((2, steps, early_pieces)),
+            pltpu.SemaphoreType.DMA((2, chips, early_pieces)),
+            pltpu.SemaphoreType.DMA((2, chips, early_pieces)),
+            pltpu.SemaphoreType.DMA((2, chips, early_pieces)),
+            pltpu.SemaphoreType.DMA((2, chips, early_pieces)),
             pltpu.SemaphoreType.DMA((tensor_count,)),
             pltpu.SemaphoreType.DMA((tensor_count,)),
             pltpu.SemaphoreType.DMA((seq_count,)),
             pltpu.SemaphoreType.DMA((seq_count,)),
         ],
         compiler_params=pltpu.CompilerParams(
-            collective_id=0, has_side_effects=True, vmem_limit_bytes=48 << 20
+            collective_id=0, has_side_effects=True, vmem_limit_bytes=60 << 20
         ),
         name="layer",
     )(*operands)
-    return (rewards[0], dx, dz, jnp.stack([db, dc], axis=1), dstep[:heads].T)
+    rewards, dx, dz, dmaps, dstep = deliver(results)
+    return (
+        rewards.reshape(tokens),
+        dx,
+        dz,
+        dmaps.reshape(tokens, 2, STATE),
+        dstep.T,
+    )
 
 
 def solution(mesh):

time: 122 us -> 97.8 us (0.80)
  Pallas kernels: 107 us -> 95.7 us
  local copies, waits for them, and re-layouts: 10.8 us -> 0 us
  other arithmetic: 3.16 us -> 1.26 us
    pallas_call x1 -> x2, Pallas kernels: 107 us -> 95.7 us  [the longest x1 93.5 us: on_device(): pl.pallas_call(layer_kernel, out_shape=(jax.ShapeDtypeStruct((1, tokens),...]
    unnamed x13 -> x0, local copies, waits for them, and re-layouts: 6.47 us -> none
    slice x2 -> x0, local copies, waits for them, and re-layouts: 2 us -> none  [the longest x1 1.4 us: on_device(): state_maps[:, 1]]
    broadcast_in_dim x5 -> x0, local copies, waits for them, and re-layouts: 1.62 us -> none  [the longest x1 0.74 us: on_device(): traj_lengths[:, None]]
    broadcast_in_dim x2 -> x0, other arithmetic: 1.61 us -> none  [the longest x1 0.81 us: on_device(): twice(step_bias)[:, None]]
    concatenate x2 -> x0, other arithmetic: 1.53 us -> none  [the longest x1 0.77 us: twice(): return jnp.concatenate([value, value], axis=0)]
    pallas_call x0 -> x1, other arithmetic: none -> 1.26 us  [deliver(): pl.pallas_call(deliver_kernel, out_shape=tuple((jax.ShapeDtypeStruct(v.sh...]
where the time goes in v1:
time: 97.8 us; the launch traced here: 97.6 us
  Pallas kernels  95.7 us (98%)
  other arithmetic  1.26 us (1%)
    pallas_call x1, Pallas kernels, on_device(): pl.pallas_call(layer_kernel, out_shape=(jax.ShapeDtypeStruct((1, tokens),...  93.5 us
    pallas_call x1, Pallas kernels, deliver(): pl.pallas_call(deliver_kernel, out_shape=tuple((jax.ShapeDtypeStruct(v.sh...  2.19 us

profile of v1, /device:TPU:15, one launch (start us, length us, event | category | flops | bytes accessed | tf_op | source)
XLA Modules:
  0.0 97.6 jit_solution(3765225016232984587)
XLA Ops:
  0.6 93.5 %layer.1 = (f32[1,384]{1,0:T(1,128)}, bf16[384,512]{1,0:T(8,128)(2,1)}, bf16[384,512]{1,0:T(8,128)(2,1)}, bf16[768,128]{1,0:T(8,128)(2,1)}, f32[4,384]{1,0:T(4,128)}) custom-call(bf16[384,512]{1,0:T(8,128)(2,1)} %x_hbm.1, bf16[384,512]{1,0:T(8,128)(2,1)} %z_hbm.1, bf16[768,128]{1,0:T(8,128)(2,1)} %bitcast.8, f32[4,384]{1,0:T(4,128)} %bitcast.11, f32[4]{0:T(128)} %bias_ref.1, ...), custom_call_target="tpu_custom_call" | custom-call | tf_op jit(solution)/shard_map/layer/pallas_call | solution.py:907
  94.2 2.2 %deliver.1 = (f32[1,384]{1,0:T(1,128)}, bf16[384,512]{1,0:T(8,128)(2,1)}, bf16[384,512]{1,0:T(8,128)(2,1)}, bf16[768,128]{1,0:T(8,128)(2,1)}, f32[4,384]{1,0:T(4,128)}) custom-call(f32[1,384]{1,0:T(1,128)} %get-tuple-element.15.refs_0_, bf16[384,512]{1,0:T(8,128)(2,1)} %get-tuple-element.16.refs_1_, bf16[384,512]{1,0:T(8,128)(2,1)} %get-tuple-element.17.refs_2_, ...), custom_call_target="tpu_custom_call" | custom-call | tf_op jit(solution)/shard_map/deliver/pallas_call | solution.py:853
  96.4 1.3 %reduce = f32[384]{0:T(512)} reduce(f32[1,384]{1,0:T(1,128)} %get-tuple-element.20, f32[]{:T(128)} %constant.4), dimensions={0}, to_apply=%get-tuple-element.20.reduce_sub_computation | reduce | bytes 3076 | tf_op jit(solution)/shard_map/deliver/pallas_call | solution.py:853

commit v2 on v1

--- a/solution.py
+++ b/solution.py
@@ -93,7 +93,17 @@
     own_stats,
     far_stats,
     own_reward,
+    state_relay_out,
+    state_relay_in,
+    grad_relay_out,
+    grad_relay_in,
+    grad_in,
+    kept,
+    facts,
+    factors,
     load_sems,
+    relay_send,
+    relay_recv,
     state_send,
     state_recv,
     grad_send,
@@ -265,6 +275,33 @@
     def grad_copy(distance):
         return far_copy(grad_out, grad_far, grad_send, grad_recv, distance, -1)
 
+    def relay_copy(buffer_out, buffer_in, send, recv, direction):
+        return pltpu.make_async_remote_copy(
+            src_ref=buffer_out,
+            dst_ref=buffer_in,
+            send_sem=send,
+            recv_sem=recv,
+            device_id=(lax.rem(seq + seq_count + direction, seq_count), tensor),
+            device_id_type=MESH,
+        )
+
+    def state_relay():
+        return relay_copy(state_relay_out, state_relay_in, relay_send.at[0], relay_recv.at[0], 1)
+
+    def grad_relay():
+        return relay_copy(grad_relay_out, grad_relay_in, relay_send.at[1], relay_recv.at[1], -1)
+
+    parity = lax.rem(seq, 2)
+
+    def for_parity(taker, copy, direction, act):
+        for kind in range(2):
+
+            @pl.when(parity == kind)
+            def _():
+                for distance in range(1, reach + 1):
+                    if (kind + direction * distance) % 2 == taker:
+                        act(copy(distance))
+
     def gathered(far):
         total, carry = None, None
         for k in range(reach):
@@ -291,8 +328,7 @@
     state_out[0:STATE] = dot(b_ref[...], weighted_x[...], TN).astype(jnp.bfloat16)
     state_out[STATE:] = through_rows
     pl.semaphore_wait(barrier, tensor_count + seq_count - 2)
-    for distance in range(1, reach + 1):
-        state_copy(distance).start()
+    for_parity(0, state_copy, 1, lambda copy: copy.start())
 
     for tb in range(blocks):
         reached = (tb + 1) * BLOCK
@@ -325,43 +361,22 @@
     loads[8].wait()
     reward_channels = jnp.sum(dot(terms, weight[...], NN), axis=0, keepdims=True)
 
-    tile = (BLOCK, BLOCK)
-    unroll = 4
-    for tb in range(blocks):
-        token = iota(tile, 0) + (seq * tokens + tb * BLOCK)
-
-        def find(i, total):
-            for k in range(unroll):
-                start = pl.multiple_of((i * unroll + k) * BLOCK, BLOCK)
-                row = pairs_ref[0:1, pl.ds(start, BLOCK)]
-                order = (iota(tile, 1) + start).astype(jnp.float32)
-                total = total + jnp.where(row == token, order, 0.0)
-            return total
-
-        zero = jnp.zeros(tile, jnp.float32)
-        order = jnp.sum(
-            lax.fori_loop(0, pair_tiles // unroll, find, zero), axis=1, keepdims=True
-        )
-        odd = order - 2.0 * jnp.floor(order * 0.5)
-        other = jnp.broadcast_to(order + 1.0 - 2.0 * odd, tile)
-
-        def fetch(i, total):
-            for k in range(unroll):
-                start = pl.multiple_of((i * unroll + k) * BLOCK, BLOCK)
-                row = pairs_ref[0:1, pl.ds(start, BLOCK)].astype(jnp.float32)
-                order = (iota(tile, 1) + start).astype(jnp.float32)
-                total = total + jnp.where(other == order, row, 0.0)
-            return total
-
-        mate = jnp.sum(
-            lax.fori_loop(0, pair_tiles // unroll, fetch, zero), axis=1, keepdims=True
-        )
-        mate_all[span(tb)] = jnp.broadcast_to(mate, tile)
-        sign_all[span(tb)] = jnp.broadcast_to(2.0 * odd - 1.0, tile)
-
-    for distance in range(1, reach + 1):
-        state_copy(distance).wait_recv()
-    state_in[...] = gathered(state_far)
+    @pl.when(parity == 0)
+    def _():
+        for distance in range(1, reach + 1):
+            state_copy(distance).wait_recv()
+        total = gathered(state_far)
+        state_in[...] = total
+        state_relay_out[...] = (
+            state_out[0:STATE].astype(jnp.float32) + through_wide * total
+        ).astype(jnp.bfloat16)
+        state_relay().start()
+
+    @pl.when(parity == 1)
+    def _():
+        state_relay().wait_recv()
+        state_in[...] = state_relay_in[...].astype(jnp.float32)
+
     incoming = state_in[...].astype(jnp.bfloat16)
     gain = gain_ref[...]
     skip = jnp.concatenate([jnp.full((1, width), skip_ref[h]) for h in range(heads)], axis=1)
@@ -383,6 +398,40 @@
         )
         _, _, _, _, gated, inverse = gating(tb)
         mixed[span(tb)] = (gated * inverse * gain).astype(jnp.bfloat16)
+
+    tile = (BLOCK, BLOCK)
+    unroll = 4
+    def search(tb):
+        token = iota(tile, 0) + (seq * tokens + tb * BLOCK)
+
+        def find(i, total):
+            for k in range(unroll):
+                start = pl.multiple_of((i * unroll + k) * BLOCK, BLOCK)
+                row = pairs_ref[0:1, pl.ds(start, BLOCK)]
+                order = (iota(tile, 1) + start).astype(jnp.float32)
+                total = total + jnp.where(row == token, order, 0.0)
+            return total
+
+        zero = jnp.zeros(tile, jnp.float32)
+        order = jnp.sum(
+            lax.fori_loop(0, pair_tiles // unroll, find, zero), axis=1, keepdims=True
+        )
+        odd = order - 2.0 * jnp.floor(order * 0.5)
+        other = jnp.broadcast_to(order + 1.0 - 2.0 * odd, tile)
+
+        def fetch(i, total):
+            for k in range(unroll):
+                start = pl.multiple_of((i * unroll + k) * BLOCK, BLOCK)
+                row = pairs_ref[0:1, pl.ds(start, BLOCK)].astype(jnp.float32)
+                order = (iota(tile, 1) + start).astype(jnp.float32)
+                total = total + jnp.where(other == order, row, 0.0)
+            return total
+
+        mate = jnp.sum(
+            lax.fori_loop(0, pair_tiles // unroll, fetch, zero), axis=1, keepdims=True
+        )
+        mate_all[span(tb)] = jnp.broadcast_to(mate, tile)
+        sign_all[span(tb)] = jnp.broadcast_to(2.0 * odd - 1.0, tile)
 
     last = chips - 2
 
@@ -554,7 +603,9 @@
         reduce_work(i)
         return 0
 
-    lax.fori_loop(0, last - 3, reduce_step, 0)
+    for tb in range(blocks):
+        reduce_step(tb, 0)
+        search(tb)
     start_halving(last + 1, own_spots)
     lax.fori_loop(last - 3, last - 1, lambda i, _: reduce_work(i) or 0, 0)
 
@@ -686,32 +737,14 @@
     own_reward[...] = jnp.broadcast_to(stats[0:1] / scale, own_reward.shape)
     rewards[seq] = own_reward[...]
 
-    def start_reward(k, _):
-        reward_copy(k).start()
-        return 0
-
-    lax.fori_loop(1, seq_count, start_reward, 0)
-    lax.fori_loop(2, last - 1, gather_step, 0)
-    for i in (last - 1, last):
-        take(i, False)
-        add_joined(i, [arrived_spot(way, i - 1) for way in range(2)])
-    add_joined(last + 1, [arrived_spot(way, last) for way in range(2)])
-
-    def end_reward(k, _):
-        reward_copy(k).wait()
-        return 0
-
-    lax.fori_loop(1, seq_count, end_reward, 0)
-
-    reward_out[...] = own_reward[0:1]
-
-    facts = jnp.concatenate(
+    facts[...] = jnp.concatenate(
         [stats, jnp.broadcast_to(scale, stats.shape), own_reward[...]]
         + [jnp.zeros((BLOCK - 24, tokens), jnp.float32)],
         axis=0,
     ).T
     lane = iota(tile, 1)
-    for tb in range(blocks):
+
+    def match(tb):
         mate = mate_all[span(tb)].astype(jnp.int32)
         sign = sign_all[span(tb), 0:1]
 
@@ -728,17 +761,53 @@
         own_scale = facts[span(tb), 8:9]
         push = sign * (facts[span(tb), 16:17] - mate_reward)
         pair_grad = sign * (loss_scale / (1.0 + jnp.exp(-push)))
+        hidden_factor = own_along / (model_width * own_scale * own_scale)
+        factors[span(tb)] = jnp.where(lane == 0, pair_grad / own_scale, hidden_factor)
+
+    def start_reward(k, _):
+        reward_copy(k).start()
+        return 0
+
+    lax.fori_loop(1, seq_count, start_reward, 0)
+    lax.fori_loop(2, last - 2, gather_step, 0)
+
+    def end_reward(k, _):
+        reward_copy(k).wait()
+        return 0
+
+    lax.fori_loop(1, seq_count, end_reward, 0)
+    match(0)
+    gather_step(last - 2, 0)
+    for i in (last - 1, last):
+        match(i - last + 2)
+        take(i, False)
+        add_joined(i, [arrived_spot(way, i - 1) for way in range(2)])
+    add_joined(last + 1, [arrived_spot(way, last) for way in range(2)])
+
+
+    reward_out[...] = own_reward[0:1]
+
+    for tb in range(blocks):
+        own_factor, hidden_factor = factors[span(tb), 0:1], factors[span(tb), 1:2]
         y, z, sig, silu, gated, inverse = gating(tb)
         d_gained = gain * (
-            (pair_grad / own_scale)
-            * (reward_channels - (own_along / (model_width * own_scale * own_scale)) * back[span(tb)])
+            own_factor * (reward_channels - hidden_factor * back[span(tb)])
         )
         shared = jnp.sum(gated * d_gained, axis=1, keepdims=True) / channels
         d_gated = inverse * d_gained - gated * (inverse * inverse * inverse * shared)
-        dz_ref[span(tb)] = (d_gated * y * (sig * (1.0 + z * (1.0 - sig)))).astype(jnp.bfloat16)
+        kept[span(tb)] = d_gated
         dy = d_gated * silu
         dy_all[span(tb)] = dy.astype(jnp.bfloat16)
         faded_dy[span(tb)] = (dy * expanded(1, tb)).astype(jnp.bfloat16)
+    grad_out[0:STATE] = dot(c_ref[...], faded_dy[...], TN).astype(jnp.bfloat16)
+    grad_out[STATE:] = through_rows
+    for_parity(1, grad_copy, -1, lambda copy: copy.start())
+
+    for tb in range(blocks):
+        y, z, d_gated = y_all[span(tb)], z_ref[span(tb)].astype(jnp.float32), kept[span(tb)]
+        sig = 1.0 / (1.0 + jnp.exp(-z))
+        dz_ref[span(tb)] = (d_gated * y * (sig * (1.0 + z * (1.0 - sig)))).astype(jnp.bfloat16)
+        dy = d_gated * (z * sig)
         dx_all[span(tb)] = skip * dy
         product = dy * carried_all[span(tb)]
         total = jnp.zeros(tile, jnp.float32)
@@ -747,11 +816,6 @@
                 lane == h, jnp.sum(product[:, lanes(h)], axis=1, keepdims=True), 0.0
             )
         sums[span(tb)] = total
-    grad_out[0:STATE] = dot(c_ref[...], faded_dy[...], TN).astype(jnp.bfloat16)
-    grad_out[STATE:] = through_rows
-    for distance in range(1, reach + 1):
-        grad_copy(distance).start()
-
     column_sums[...] = jnp.zeros_like(column_sums)
     db_all[...] = jnp.zeros_like(db_all)
     for tb in range(blocks):
@@ -777,9 +841,23 @@
         ) + dot(faded_dy[span(tb)], incoming, NT)
         db_all[0:reached] += dot(d_score, c_ref[span(tb)], TN)
 
-    for distance in range(1, reach + 1):
-        grad_copy(distance).wait_recv()
-    grad_end = gathered(grad_far)
+    @pl.when(parity == 1)
+    def _():
+        for distance in range(1, reach + 1):
+            grad_copy(distance).wait_recv()
+        total = gathered(grad_far)
+        grad_in[...] = total
+        grad_relay_out[...] = (
+            grad_out[0:STATE].astype(jnp.float32) + through_wide * total
+        ).astype(jnp.bfloat16)
+        grad_relay().start()
+
+    @pl.when(parity == 0)
+    def _():
+        grad_relay().wait_recv()
+        grad_in[...] = grad_relay_in[...].astype(jnp.float32)
+
+    grad_end = grad_in[...]
     crossing = jnp.sum(grad_end * state_in[...], axis=0, keepdims=True)
     grad_end = grad_end.astype(jnp.bfloat16)
     for tb in range(blocks):
@@ -811,9 +889,16 @@
     d_step = (column_sums[...] + weight_sums) / step - rate * d_exponent
     dstep_ref[...] = (d_step / (1.0 + jnp.exp(-pre)))[0:heads]
 
-    for distance in range(1, reach + 1):
-        state_copy(distance).wait_send()
-        grad_copy(distance).wait_send()
+    for_parity(0, state_copy, 1, lambda copy: copy.wait_send())
+    for_parity(1, grad_copy, -1, lambda copy: copy.wait_send())
+
+    @pl.when(parity == 0)
+    def _():
+        state_relay().wait_send()
+
+    @pl.when(parity == 1)
+    def _():
+        grad_relay().wait_send()
 
     def end_stats(k, _):
         stats_copy(k).wait_send()
@@ -845,14 +930,16 @@
 def deliver_kernel(*refs):
     count = len(refs) // 2
     for source, target in zip(refs[:count], refs[count:]):
-        target[...] = source[...]
+        target[...] = source[...].reshape(target.shape)
 
 
 def deliver(values):
     vmem = pl.BlockSpec(memory_space=pltpu.VMEM)
     return pl.pallas_call(
         deliver_kernel,
-        out_shape=tuple(jax.ShapeDtypeStruct(v.shape, v.dtype) for v in values),
+        out_shape=tuple(
+            jax.ShapeDtypeStruct(v.shape[1:] if v.shape[0] == 1 else v.shape, v.dtype) for v in values
+        ),
         in_specs=[vmem] * len(values),
         out_specs=(vmem,) * len(values),
         compiler_params=pltpu.CompilerParams(vmem_limit_bytes=60 << 20),
@@ -963,7 +1050,17 @@
             pltpu.VMEM((8, tokens), f32),
             pltpu.VMEM((tensor_count, 8, tokens), f32),
             pltpu.VMEM((8, tokens), f32),
+            pltpu.VMEM((STATE, channels), bf16),
+            pltpu.VMEM((STATE, channels), bf16),
+            pltpu.VMEM((STATE, channels), bf16),
+            pltpu.VMEM((STATE, channels), bf16),
+            pltpu.VMEM((STATE, channels), f32),
+            pltpu.VMEM((tokens, channels), f32),
+            pltpu.VMEM((tokens, BLOCK), f32),
+            pltpu.VMEM((tokens, BLOCK), f32),
             pltpu.SemaphoreType.DMA((9,)),
+            pltpu.SemaphoreType.DMA((2,)),
+            pltpu.SemaphoreType.DMA((2,)),
             pltpu.SemaphoreType.DMA((reach,)),
             pltpu.SemaphoreType.DMA((reach,)),
             pltpu.SemaphoreType.DMA((reach,)),
@@ -994,7 +1091,7 @@
     )(*operands)
     rewards, dx, dz, dmaps, dstep = deliver(results)
     return (
-        rewards.reshape(tokens),
+        rewards,
         dx,
         dz,
         dmaps.reshape(tokens, 2, STATE),

time: 97.8 us -> 92.9 us (0.950)
  Pallas kernels: 95.7 us -> 91.4 us
  other arithmetic: 1.26 us -> 0 us
    pallas_call x1, Pallas kernels: 93.5 us -> 89.2 us  [on_device(): pl.pallas_call(layer_kernel, out_shape=(jax.ShapeDtypeStruct((1, tokens),...]
    pallas_call x1 -> x0, other arithmetic: 1.26 us -> none  [deliver(): pl.pallas_call(deliver_kernel, out_shape=tuple((jax.ShapeDtypeStruct(v.sh...]
where the time goes in v2:
time: 92.9 us; the launch traced here: 92.1 us
  Pallas kernels  91.4 us (98%)
    pallas_call x1, Pallas kernels, on_device(): pl.pallas_call(layer_kernel, out_shape=(jax.ShapeDtypeStruct((1, tokens),...  89.2 us
    pallas_call x1, Pallas kernels, deliver(): pl.pallas_call(deliver_kernel, out_shape=tuple((jax.ShapeDtypeStruct(v.sh...  2.19 us

profile of v2, /device:TPU:15, one launch (start us, length us, event | category | flops | bytes accessed | tf_op | source)
XLA Modules:
  0.0 92.1 jit_solution(2518119057444194281)
XLA Ops:
  0.6 89.2 %layer.1 = (f32[1,384]{1,0:T(1,128)}, bf16[384,512]{1,0:T(8,128)(2,1)}, bf16[384,512]{1,0:T(8,128)(2,1)}, bf16[768,128]{1,0:T(8,128)(2,1)}, f32[4,384]{1,0:T(4,128)}) custom-call(bf16[384,512]{1,0:T(8,128)(2,1)} %x_hbm.1, bf16[384,512]{1,0:T(8,128)(2,1)} %z_hbm.1, bf16[768,128]{1,0:T(8,128)(2,1)} %bitcast.8, f32[4,384]{1,0:T(4,128)} %bitcast.11, f32[4]{0:T(128)} %bias_ref.1, ...), custom_call_target="tpu_custom_call" | custom-call | tf_op jit(solution)/shard_map/layer/pallas_call | solution.py:994
  89.9 2.2 %deliver.1 = (f32[384]{0:T(512)}, bf16[384,512]{1,0:T(8,128)(2,1)}, bf16[384,512]{1,0:T(8,128)(2,1)}, bf16[768,128]{1,0:T(8,128)(2,1)}, f32[4,384]{1,0:T(4,128)}) custom-call(f32[1,384]{1,0:T(1,128)} %get-tuple-element.15.refs_0_, bf16[384,512]{1,0:T(8,128)(2,1)} %get-tuple-element.16.refs_1_, bf16[384,512]{1,0:T(8,128)(2,1)} %get-tuple-element.17.refs_2_, ...), custom_call_target="tpu_custom_call" | custom-call | tf_op jit(solution)/shard_map/deliver/pallas_call | solution.py:938

commit v3 on v2

--- a/solution.py
+++ b/solution.py
@@ -26,6 +26,18 @@
 
 def iota(shape, axis):
     return lax.broadcasted_iota(jnp.int32, shape, axis)
+
+
+def three_terms(value):
+    high = value.astype(jnp.bfloat16).astype(jnp.float32)
+    rest = value - high
+    middle = rest.astype(jnp.bfloat16).astype(jnp.float32)
+    return jnp.concatenate([high, middle, rest - middle], axis=0).astype(jnp.bfloat16)
+
+
+def exact_dot(value, right, dims):
+    result = dot(three_terms(value), right, dims)
+    return result[0:8] + result[8:16] + result[16:24]
 
 
 def layer_kernel(
@@ -197,8 +209,8 @@
     step = jnp.maximum(pre, 0.0) + jnp.log1p(jnp.exp(-jnp.abs(pre)))
     exponent = -step * rate
     square = (tokens, tokens)
-    upto = (iota(square, 0) <= iota(square, 1)).astype(jnp.float32)
-    cumulative = dot(exponent, upto, NN, HIGH)
+    upto = jnp.where(iota(square, 0) <= iota(square, 1), 1.0, 0.0).astype(jnp.bfloat16)
+    cumulative = exact_dot(exponent, upto, NN)
     count = length_ref.shape[1]
     openings = jnp.sum(
         jnp.where(
@@ -531,7 +543,8 @@
     early_turns = [(j, way) for j in range(early_pieces) for way in range(2)]
 
     def cut_piece(value, j):
-        return value[j * piece : (j + 1) * piece]
+        rows = value.shape[0] // (late_pieces if value.shape[1] == late_width else early_pieces)
+        return value[j * rows : (j + 1) * rows]
 
     def start_halving(i, at=None):
         for way in range(2):
@@ -565,9 +578,7 @@
     start_halving(3)
     start_early(1)
 
-    along = dot(
-        jnp.broadcast_to(reward_channels, (8, channels)), mixed[...].astype(jnp.float32), NT, HIGH
-    )
+    along = exact_dot(jnp.broadcast_to(reward_channels, (8, channels)), mixed[...], NT)
 
     own_spots = [(place, way) for way in range(2)]
 
@@ -884,8 +895,8 @@
     d_last = jnp.sum(weight_sums, axis=1, keepdims=True) + through * reach_end
     d_cumulative = turned[0:8] - column_sums[...] - weight_sums
     d_cumulative = d_cumulative + jnp.where(iota(step.shape, 1) == tokens - 1, d_last, 0.0)
-    onward = (iota(square, 0) >= iota(square, 1)).astype(jnp.float32)
-    d_exponent = dot(d_cumulative, onward, NN, HIGH)
+    onward = jnp.where(iota(square, 0) >= iota(square, 1), 1.0, 0.0).astype(jnp.bfloat16)
+    d_exponent = exact_dot(d_cumulative, onward, NN)
     d_step = (column_sums[...] + weight_sums) / step - rate * d_exponent
     dstep_ref[...] = (d_step / (1.0 + jnp.exp(-pre)))[0:heads]
 
@@ -969,7 +980,7 @@
     late_width = model_width // (2 * chips)
     early_width = late_width // 2
     late_pieces, early_pieces = 1, 1
-    piece = tokens // (late_pieces + early_pieces)
+    piece = tokens * 10 // 24
     steps = chips - 1
     reach = -(-(longest - 1) // tokens)
     bf16, f32 = jnp.bfloat16, jnp.float32
@@ -1042,11 +1053,11 @@
             pltpu.VMEM((2, late_pieces, piece, late_width), bf16),
             pltpu.VMEM((2, late_pieces, piece, late_width), bf16),
             pltpu.VMEM((chips, 2, late_pieces, piece, late_width), bf16),
-            pltpu.VMEM((2, steps, early_pieces, piece, early_width), bf16),
-            pltpu.VMEM((2, steps, early_pieces, piece, early_width), bf16),
-            pltpu.VMEM((2, chips, early_pieces, piece, early_width), bf16),
-            pltpu.VMEM((2, chips, early_pieces, piece, early_width), bf16),
-            pltpu.VMEM((chips, 2, 2, early_pieces, piece, early_width), bf16),
+            pltpu.VMEM((2, steps, early_pieces, tokens - piece, early_width), bf16),
+            pltpu.VMEM((2, steps, early_pieces, tokens - piece, early_width), bf16),
+            pltpu.VMEM((2, chips, early_pieces, tokens - piece, early_width), bf16),
+            pltpu.VMEM((2, chips, early_pieces, tokens - piece, early_width), bf16),
+            pltpu.VMEM((chips, 2, 2, early_pieces, tokens - piece, early_width), bf16),
             pltpu.VMEM((8, tokens), f32),
             pltpu.VMEM((tensor_count, 8, tokens), f32),
             pltpu.VMEM((8, tokens), f32),

time: 92.9 us -> 92.1 us (level)
  Pallas kernels: 91.4 us -> 90.4 us
    pallas_call x1, Pallas kernels: 89.2 us -> 88.2 us  [on_device(): pl.pallas_call(layer_kernel, out_shape=(jax.ShapeDtypeStruct((1, tokens),...]
where the time goes in v3:
time: 92.1 us; the launch traced here: 91 us
  Pallas kernels  90.4 us (98%)
    pallas_call x1, Pallas kernels, on_device(): pl.pallas_call(layer_kernel, out_shape=(jax.ShapeDtypeStruct((1, tokens),...  88.2 us
    pallas_call x1, Pallas kernels, deliver(): pl.pallas_call(deliver_kernel, out_shape=tuple((jax.ShapeDtypeStruct(v.sh...  2.19 us

profile of v3, /device:TPU:15, one launch (start us, length us, event | category | flops | bytes accessed | tf_op | source)
XLA Modules:
  0.0 91.0 jit_solution(2907403063969968543)
XLA Ops:
  0.6 88.2 %layer.1 = (f32[1,384]{1,0:T(1,128)}, bf16[384,512]{1,0:T(8,128)(2,1)}, bf16[384,512]{1,0:T(8,128)(2,1)}, bf16[768,128]{1,0:T(8,128)(2,1)}, f32[4,384]{1,0:T(4,128)}) custom-call(bf16[384,512]{1,0:T(8,128)(2,1)} %x_hbm.1, bf16[384,512]{1,0:T(8,128)(2,1)} %z_hbm.1, bf16[768,128]{1,0:T(8,128)(2,1)} %bitcast.8, f32[4,384]{1,0:T(4,128)} %bitcast.11, f32[4]{0:T(128)} %bias_ref.1, ...), custom_call_target="tpu_custom_call" | custom-call | tf_op jit(solution)/shard_map/layer/pallas_call | solution.py:1005
  88.8 2.2 %deliver.1 = (f32[384]{0:T(512)}, bf16[384,512]{1,0:T(8,128)(2,1)}, bf16[384,512]{1,0:T(8,128)(2,1)}, bf16[768,128]{1,0:T(8,128)(2,1)}, f32[4,384]{1,0:T(4,128)}) custom-call(f32[1,384]{1,0:T(1,128)} %get-tuple-element.15.refs_0_, bf16[384,512]{1,0:T(8,128)(2,1)} %get-tuple-element.16.refs_1_, bf16[384,512]{1,0:T(8,128)(2,1)} %get-tuple-element.17.refs_2_, ...), custom_call_target="tpu_custom_call" | custom-call | tf_op jit(solution)/shard_map/deliver/pallas_call | solution.py:949
